TPU v7x, 512 devices: a whole 4x8x8 slice. The times are simulated.
512 devices in a mesh: band: 16 (over y, core), ma: 32 (over z, x).
Axes of the slice: x: 4, y: 8, z: 8, core: 2. Of those that a mesh axis runs over, the one named last changes fastest.
Arguments:
- coeffs: bfloat16 [64, 2048, 48], P('ma'), may hold values from -6 to 6
- tables: bfloat16 [64, 2, 256, 2048], P('ma'), may hold values from -0.005859375 to 0.005859375
- beam: float32 [16, 2048], P('band'), may hold values from 0.2 to 1
- mixing: float32 [16, 3, 256, 4096], P('band', None, 'ma'), may hold values from 0.3 to 1.5
- noise_diag: float32 [16, 2, 256, 4096], P('band', None, 'ma'), may hold values from 0.05 to 0.2
- noise_cross: float32 [16, 256, 4096], P('band', 'ma'), may hold values from -0.04 to 0.04
- prior: float32 [6, 2048], P(None, 'band'), may hold values from 0.3 to 3
- m_values: int32 [64], replicated, may hold values from 0 to 63, as said below
- cycle_ids: int32 [256], P('ma'), may hold values from 0 to 255, each once
Outputs:
- product: float32 [64, 2048, 48], P('ma', 'band')
Inputs may be any that keep to these rules, and one draw needn't show every extreme that they name: `m_values`: each of 0 to 63 appears once; slots 2k and 2k + 1 hold m and 63 - m. `cycle_ids`: each cycle number appears once.
All inputs are finite; a program needn't handle non-finite values.
Results may differ from a plain program's by a relative error of at most 0.0015.
Values may be sent and summed in bfloat16 or wider, within the bound.
No kernel may reach another device: no remote copies, remote signals or barrier semaphores. Data moves between devices by JAX's collectives and lax.ppermute only.
A program may use at most 64 MiB of HBM per device.

v0:
```python
import jax
import jax.numpy as jnp
from jax import lax
from jax.sharding import PartitionSpec as P

PIX = 4096
COMPS = 3


def combine_pairs(plain_part, crossed):
    dims_all = plain_part.shape
    plain_part = plain_part.reshape(dims_all[:-1] + (dims_all[-1] // 4, 4))
    crossed = crossed.reshape(dims_all[:-1] + (dims_all[-1] // 4, 4))
    combined = jnp.stack(
        [
            plain_part[..., 0] - crossed[..., 3],
            plain_part[..., 1] + crossed[..., 2],
            plain_part[..., 2] + crossed[..., 1],
            plain_part[..., 3] - crossed[..., 0],
        ],
        axis=-1,
    )
    return combined.reshape(dims_all)


def trig_table(mode_ids, parity, pixels):
    offsets = 2 * jnp.arange(pixels, dtype=jnp.int32) + parity
    phase_index = mode_ids[:, None] * offsets[None, :] % (2 * pixels)
    angles = jnp.pi * phase_index.astype(jnp.float32) / pixels
    weight = jnp.where(mode_ids == 0, 1.0, 2.0).astype(jnp.float32)[:, None]
    return jnp.concatenate([weight * jnp.cos(angles), -weight * jnp.sin(angles)], 0).astype(
        jnp.bfloat16
    )


def on_device(coeffs, tables, beam, mixing, noise_diag, noise_cross, prior, m_values, cycle_ids):
    beamed = (coeffs.astype(jnp.float32) * beam[0][None, :, None]).astype(jnp.bfloat16)
    table_even = trig_table(m_values, 0, PIX)
    table_odd = trig_table(m_values, 1, PIX)
    cycle_tables = jnp.where((cycle_ids % 2 == 1)[:, None, None], table_odd[None], table_even[None])
    mix_local = mixing[0].transpose(1, 0, 2)
    diag_local = noise_diag[0].transpose(1, 0, 2)
    cross_local = noise_cross[0]
    stacked = jnp.einsum("mtrl,mlc->mtrc", tables, beamed, preferred_element_type=jnp.float32)
    spectra = combine_pairs(stacked[:, 0], stacked[:, 1]).astype(jnp.bfloat16)
    exchanged = lax.all_to_all(spectra, "ma", split_axis=1, concat_axis=0, tiled=True)
    mode_count, cycle_count, width = exchanged.shape
    fields = width // 2
    flattened = exchanged.reshape(mode_count, cycle_count, fields, 2).transpose(1, 2, 3, 0)
    flattened = flattened.reshape(cycle_count, fields, 2 * mode_count)
    pixel_maps = jnp.einsum(
        "rfj,rjp->rfp", flattened, cycle_tables, preferred_element_type=jnp.float32
    )
    pixel_maps = pixel_maps.reshape(cycle_count, fields // (2 * COMPS), COMPS, 2, PIX)
    sky_map = jnp.sum(pixel_maps * mix_local[:, None, :, None, :], axis=2)
    weighted_q = (
        diag_local[:, 0][:, None] * sky_map[:, :, 0] + cross_local[:, None] * sky_map[:, :, 1]
    )
    weighted_u = (
        cross_local[:, None] * sky_map[:, :, 0] + diag_local[:, 1][:, None] * sky_map[:, :, 1]
    )
    weighted = jnp.stack([weighted_q, weighted_u], 2)
    returned_map = (weighted[:, :, None] * mix_local[:, None, :, None, :]).astype(jnp.bfloat16)
    returned_map = returned_map.reshape(cycle_count, fields, PIX)
    returned = jnp.einsum(
        "rfp,rjp->rfj", returned_map, cycle_tables, preferred_element_type=jnp.float32
    )
    returned = returned.astype(jnp.bfloat16).reshape(cycle_count, fields, 2, mode_count)
    returned = returned.transpose(3, 0, 1, 2).reshape(mode_count, cycle_count, width)
    arrived = lax.all_to_all(returned, "ma", split_axis=0, concat_axis=1, tiled=True)
    plain_part = jnp.einsum(
        "mrl,mrc->mlc", tables[:, 0], arrived, preferred_element_type=jnp.float32
    )
    crossed = jnp.einsum("mrl,mrc->mlc", tables[:, 1], arrived, preferred_element_type=jnp.float32)
    partial_sum = combine_pairs(plain_part, crossed)
    partial_sum = partial_sum * beam[0][None, :, None]
    share_len = partial_sum.shape[1] // lax.axis_size("band")
    offset = lax.axis_index("band") * share_len
    local_sum = lax.psum_scatter(partial_sum, "band", scatter_dimension=1, tiled=True)
    coeff_share = lax.dynamic_slice_in_dim(coeffs, offset, share_len, 1).astype(jnp.float32)
    chain_count = coeffs.shape[2] // (4 * COMPS)
    prior_cols = prior.reshape(COMPS, 2, share_len).transpose(2, 0, 1)
    prior_cols = jnp.broadcast_to(
        prior_cols[:, None, :, :, None], (share_len, chain_count, COMPS, 2, 2)
    )
    prior_cols = prior_cols.reshape(share_len, coeffs.shape[2])
    return local_sum + prior_cols[None] * coeff_share


def solution(mesh):
    in_specs = (
        P("ma", None, None),
        P("ma", None, None, None),
        P("band", None),
        P("band", None, "ma", None),
        P("band", None, "ma", None),
        P("band", "ma", None),
        P(None, "band"),
        P(),
        P("ma"),
    )
    out_specs = P("ma", "band", None)
    return jax.shard_map(
        on_device, mesh=mesh, in_specs=in_specs, out_specs=out_specs, check_vma=False
    )
```

profile of v0, /device:TPU:1, one launch (start us, length us, event | category | flops | bytes accessed | tf_op | source)
XLA Modules:
  0.0 145.6 jit_solution(14004818628999831664)
XLA Ops:
  6.5 3.7 %convolution_bitcast_fusion.2 = f32[2,2,256,48]{2,3,1,0:T(8,128)S(1)} fusion(bf16[2,2,256,2048]{3,2,1,0:T(8,128)(2,1)} %param.10, bf16[2,2048,48]{1,2,0:T(8,128)(2,1)} %param.9, f32[2048]{0:T(1024)} %bitcast.82), kind=kOutput, calls=%fused_computation.28 | convolution fusion | flops 201916416 | bytes 4792320 | tf_op jit(solution)/shard_map/mtrl,mlc->mtrc/dot_general | solution.py:44
  10.8 0.8 reshape.157
  11.6 13.7 %all-to-all-start = ((bf16[32,2,384]{2,1,0:T(2,128)(2,1)}), bf16[32,2,384]{2,1,0:T(2,128)(2,1)S(1)}, u32[]{:S(2)}, u32[]{:S(2)}) async-start(bf16[32,2,384]{2,1,0:T(2,128)(2,1)} %reshape.157), calls=%async_computation | async-start | bytes 98304 | tf_op jit(solution)/shard_map/all_to_all | solution.py:46
  25.5 8.5 %multiply_convert_fusion.2 = (bf16[64,4096]{1,0:T(8,128)(2,1)S(1)}, bf16[64,4096]{1,0:T(8,128)(2,1)S(1)}, bf16[64,4096]{1,0:T(8,128)(2,1)S(1)}, bf16[64,4096]{1,0:T(8,128)(2,1)S(1)}) fusion(s32[4096]{0:T(1024)S(1)} %iota_multiply_fusion, s32[64]{0:T(128)S(1)} %copy-done.8, f32[64]{0:T(128)S(1)} %get-tuple-element.25, f32[64]{0:T(128)S(1)} %get-tuple-element.26, ...), kind=kLoop, calls=%fused_computation.40 | loop fusion | flops 9437184 | bytes 2130688 | tf_op jit(solution)/shard_map/convert
  34.2 1.4 copy.76
  35.8 0.4 copy.74
  36.1 0.8 copy.75
  37.1 3.0 %fusion.2 = f32[8,24,4096]{2,1,0:T(8,128)} fusion(bf16[8,24,128]{2,1,0:T(8,128)(2,1)S(1)} %reshape.148, pred[8]{0:T(512)(128)(4,1)S(1)} %fusion.34, bf16[128,4096]{1,0:T(8,128)(2,1)S(1)} %get-tuple-element.28, bf16[128,4096]{1,0:T(8,128)(2,1)S(1)} %get-tuple-element.27), kind=kOutput, calls=%fused_computation.2 | convolution fusion | flops 205520896 | bytes 5292040 | tf_op jit(solution)/shard_map/rfj,rjp->rfp/dot_general | solution.py:51
  40.1 3.9 %reshape.149 = f32[8,4,3,2,4096]{4,3,2,1,0:T(2,128)S(1)} reshape(f32[8,24,4096]{2,1,0:T(8,128)} %fusion.2) | data formatting | bytes 6291456 | tf_op jit(solution)/shard_map/reshape | solution.py:54
  44.0 3.5 %multiply_reduce_fusion = f32[8,4,2,4096]{3,2,1,0:T(2,128)S(1)} fusion(f32[8,4,3,2,4096]{4,3,2,1,0:T(2,128)S(1)} %reshape.149, f32[8,3,4096]{2,1,0:T(4,128)} %copy.76), kind=kLoop, calls=%fused_computation.11 | loop fusion | flops 1310720 | bytes 4587520 | tf_op jit(solution)/shard_map/reduce_sum | solution.py:55
  47.5 1.2 multiply_add_fusion.1
  48.7 1.0 pad_maximum_fusion.2
  49.7 1.7 %multiply_convert_fusion = bf16[8,4,3,2,4096]{4,3,2,1,0:T(2,128)(2,1)S(1)} fusion(f32[8,4,2,4096]{3,2,1,0:T(2,128)S(1)} %pad_maximum_fusion.2, f32[8,3,4096]{2,1,0:T(4,128)S(1)} %copy-done), kind=kLoop, calls=%fused_computation.10 | loop fusion | flops 1572864 | bytes 3014656 | tf_op jit(solution)/shard_map/convert_element_type | solution.py:63
  51.5 0.6 convert_element_type.53
  52.1 3.9 %fusion.14 = bf16[8,24,128]{2,1,0:T(8,128)(2,1)S(1)} fusion(bf16[8,24,4096]{2,1,0:T(8,128)(2,1)S(1)} %convert_element_type.53, pred[8]{0:T(512)(128)(4,1)S(1)} %fusion.34, bf16[128,4096]{1,0:T(8,128)(2,1)} %copy-done.2, bf16[128,4096]{1,0:T(8,128)(2,1)} %copy-done.1), kind=kOutput, calls=%fused_computation.29 | convolution fusion | flops 205545472 | bytes 3719176 | tf_op jit(solution)/shard_map/rfp,rjp->rfj/dot_general | solution.py:65
  56.6 17.8 %all_to_all.33 = bf16[32,2,384]{2,1,0:T(2,128)(2,1)S(1)} all-to-all(bf16[32,2,384]{2,1,0:T(2,128)(2,1)S(1)} %reshape.159), channel_id=1, replica_groups=mesh['band'=16,'ma'=32] {'ma'}, dimensions={0} | all-to-all | bytes 98304 | tf_op jit(solution)/shard_map/all_to_all | solution.py:70
  74.5 2.1 %convolution_bitcast_fusion.1 = f32[2,2048,48]{1,2,0:T(8,128)S(1)} fusion(bf16[2,2,256,2048]{3,2,1,0:T(8,128)(2,1)} %param.10, bf16[2,32,8,48]{3,2,0,1:T(8,128)(2,1)S(1)} %bitcast.69), kind=kOutput, calls=%fused_computation.13 | convolution fusion | flops 100663296 | bytes 2932736 | tf_op jit(solution)/shard_map/mrl,mrc->mlc/dot_general | solution.py:71
  76.6 2.1 %convolution_bitcast_fusion = f32[2,2048,48]{1,2,0:T(8,128)S(1)} fusion(bf16[2,2,256,2048]{3,2,1,0:T(8,128)(2,1)} %param.10, bf16[2,32,8,48]{3,2,0,1:T(8,128)(2,1)S(1)} %bitcast.70), kind=kOutput, calls=%fused_computation.12 | convolution fusion | flops 100663296 | bytes 2932736 | tf_op jit(solution)/shard_map/mrl,mrc->mlc/dot_general | solution.py:74
  79.2 0.9 slice_subtract_fusion.1
  80.1 0.7 pad_maximum_fusion.3
  80.8 0.3 reshape.154
  81.1 1.0 broadcast_multiply_fusion
  82.1 55.2 %reduce-scatter.2.cloned.1.call-done = f32[2,128,48]{1,2,0:T(8,128)} async-done(((f32[2,2048,48]{1,2,0:T(8,128)}), f32[2,128,48]{1,2,0:T(8,128)}) %reduce-scatter.2.cloned.1.call-update) | async-done | bytes 49168 | tf_op jit(solution)/shard_map/reduce_scatter | solution.py:79
  137.4 1.4 multiply_add_fusion.2
  (47 shorter events, 2.1 us)
Async XLA Ops:
  6.5 18.8 %copy-start.8 = (s32[64]{0:T(128)S(1)}, s32[64]{0:T(128)}, u32[]{:S(2)}) copy-start(s32[64]{0:T(128)} %param.16) | copy-start | bytes 772
  6.5 18.9 %copy-start.4 = (f32[1,2,8,4096]{3,2,1,0:T(8,128)S(1)}, f32[1,2,8,4096]{3,2,1,0:T(8,128)}, u32[]{:S(2)}) copy-start(f32[1,2,8,4096]{3,2,1,0:T(8,128)} %param.13) | copy-start | bytes 786436
  11.6 24.0 %all-to-all-start = ((bf16[32,2,384]{2,1,0:T(2,128)(2,1)}), bf16[32,2,384]{2,1,0:T(2,128)(2,1)S(1)}, u32[]{:S(2)}, u32[]{:S(2)}) async-start(bf16[32,2,384]{2,1,0:T(2,128)(2,1)} %reshape.157), calls=%async_computation | async-start | bytes 98304 | tf_op jit(solution)/shard_map/all_to_all | solution.py:46
  25.3 112.1 %reduce-scatter.2.cloned.1.call-start = ((), (), s32[]{:S(2)}) async-start(), calls=%async_computation.3 | async-start | bytes 835584 | tf_op jit(solution)/shard_map/reduce_scatter | solution.py:79
  25.4 8.7 %copy-start.9 = (s32[8]{0:T(128)S(1)}, s32[8]{0:T(128)}, u32[]{:S(2)}) copy-start(s32[8]{0:T(128)} %param.17) | copy-start | bytes 100
  25.4 8.8 %copy-start.3 = (f32[1,3,8,4096]{3,2,1,0:T(8,128)S(1)}, f32[1,3,8,4096]{3,2,1,0:T(8,128)}, u32[]{:S(2)}) copy-start(f32[1,3,8,4096]{3,2,1,0:T(8,128)} %param.12) | copy-start | bytes 1179652
  34.2 2.9 %copy-start.1 = (bf16[128,4096]{1,0:T(8,128)(2,1)}, bf16[128,4096]{1,0:T(8,128)(2,1)S(1)}, u32[]{:S(2)}) copy-start(bf16[128,4096]{1,0:T(8,128)(2,1)S(1)} %get-tuple-element.27) | copy-start | bytes 3145732
  34.2 2.9 %copy-start.2 = (bf16[128,4096]{1,0:T(8,128)(2,1)}, bf16[128,4096]{1,0:T(8,128)(2,1)S(1)}, u32[]{:S(2)}) copy-start(bf16[128,4096]{1,0:T(8,128)(2,1)S(1)} %get-tuple-element.28) | copy-start | bytes 3145732
  44.0 3.5 %copy-start.5 = (f32[1,8,4096]{2,1,0:T(8,128)S(1)}, f32[1,8,4096]{2,1,0:T(8,128)}, u32[]{:S(2)}) copy-start(f32[1,8,4096]{2,1,0:T(8,128)} %param.14) | copy-start | bytes 393220
  47.4 2.3 %copy-start = (f32[8,3,4096]{2,1,0:T(4,128)S(1)}, f32[8,3,4096]{2,1,0:T(4,128)}, u32[]{:S(2)}) copy-start(f32[8,3,4096]{2,1,0:T(4,128)} %copy.76) | copy-start | bytes 1179652
  79.2 1.9 %copy-start.6 = (f32[1,2048]{1,0:T(1,128)S(1)}, f32[1,2048]{1,0:T(1,128)}, u32[]{:S(2)}) copy-start(f32[1,2048]{1,0:T(1,128)} %param.11) | copy-start | bytes 24580
  80.1 2.0 %copy-start.7 = (f32[6,128]{1,0:T(8,128)S(1)}, f32[6,128]{1,0:T(8,128)}, u32[]{:S(2)}) copy-start(f32[6,128]{1,0:T(8,128)} %param.15) | copy-start | bytes 9220
Sparse Core Ops, SparseCore 0:
  82.2 55.1 reduce-scatter.1
where the time goes:
time: 147 us; the launch traced here: 146 us
  waiting for transfers between devices  55.3 us (38%)
  other arithmetic  20.2 us (14%)
  blocking collectives  17.8 us (12%)
  matrix products  14.9 us (10%)
  between operations  13.8 us (9%)
  starting transfers between devices  13.7 us (9%)
  local copies, waits for them, and re-layouts  9.93 us (7%)
    reduce_scatter x1, waiting for transfers between devices, on_device(): lax.psum_scatter(partial_sum, 'band', scatter_dimension=1, tiled=True)  55.2 us
    all_to_all x1, blocking collectives, on_device(): lax.all_to_all(returned, 'ma', split_axis=0, concat_axis=1, tiled=True)  17.8 us
    all_to_all x1, starting transfers between devices, on_device(): lax.all_to_all(spectra, 'ma', split_axis=1, concat_axis=0, tiled=True)  13.7 us
    another operation x2, other arithmetic  8.59 us
    dot_general x1, matrix products, on_device(): jnp.einsum('rfp,rjp->rfj', returned_map, cycle_tables, preferred_element_...  3.94 us
    reshape x1, local copies, waits for them, and re-layouts, on_device(): pixel_maps.reshape(cycle_count, fields // (2 * COMPS), COMPS, 2, PIX)  3.88 us
    dot_general x1, matrix products, on_device(): jnp.einsum('mtrl,mlc->mtrc', tables, beamed, preferred_element_type=jnp.f...  3.74 us
    reduce_sum x1, other arithmetic, on_device(): sky_map = jnp.sum(pixel_maps * mix_local[:, None, :, None, :], axis=2)  3.47 us
  transfers between devices with their start and end apart: 2, of which 1 were waited for; matrix products, arithmetic and copies ran while one was open for 7% of the time, Pallas kernels for 0%

commit v1 on v0

v1 whole, which is shorter than its diff:
```python
import math

import jax
import jax.numpy as jnp
from jax import lax
from jax.experimental import pallas as pl
from jax.experimental.pallas import tpu as pltpu
from jax.sharding import Mesh
from jax.sharding import PartitionSpec as P

F32 = jnp.float32
BF16 = jnp.bfloat16

PIX = 4096
COMPS = 3
CHAINS = 4
PAIRS = CHAINS * COMPS
COLS = 4 * PAIRS
SLOT = 16
PER = 8
PLACE = (0, 2, 1, 3)

NT = (((1,), (1,)), ((), ()))
NN = (((1,), (0,)), ((), ()))


def dot(a, b, dims):
    return lax.dot_general(a, b, dims, preferred_element_type=F32)


def crossed(slots):
    return [-slots[3], slots[2], slots[1], -slots[0]]


def synth_kernel(coef_ref, tab_ref, beam_ref, out_ref, nat_ref, acc_ref):
    step = pl.program_id(0)

    @pl.when(step == 0)
    def _():
        nat_ref[...] = jnp.zeros_like(nat_ref)

    total = None
    for s in range(2):
        beamed = (coef_ref[s].astype(F32) * beam_ref[...]).astype(BF16)
        tiles = range(beamed.shape[1] // 128)
        for j in tiles:
            nat_ref[s, j, :COLS, :] = beamed[:, j * 128 : (j + 1) * 128].astype(F32)
        slots = [
            jnp.concatenate([nat_ref[s, j, pl.ds(p, SLOT, stride=4), :] for j in tiles], 1)
            for p in PLACE
        ]
        none = jnp.zeros((4 * SLOT, beamed.shape[1]), BF16)
        for which, rows in enumerate((slots, crossed(slots))):
            rows = jnp.concatenate(rows, 0).astype(BF16)
            rows = jnp.concatenate([rows, none] if s == 0 else [none, rows], 0)
            part = dot(tab_ref[s, which], rows, NT)
            total = part if total is None else total + part

    @pl.when(step == 0)
    def _():
        acc_ref[...] = total

    @pl.when(step > 0)
    def _():
        acc_ref[...] += total

    @pl.when(step == pl.num_programs(0) - 1)
    def _():
        out_ref[...] = acc_ref[...].astype(BF16)


def synth(coeffs_t, tables, beam, chunks=4):
    _, cols, levels = coeffs_t.shape
    cycles = tables.shape[2]
    width = levels // chunks
    return pl.pallas_call(
        synth_kernel,
        out_shape=jax.ShapeDtypeStruct((cycles, 128), BF16),
        grid=(chunks,),
        in_specs=[
            pl.BlockSpec((2, cols, width), lambda k: (0, 0, k)),
            pl.BlockSpec((2, 2, cycles, width), lambda k: (0, 0, 0, k)),
            pl.BlockSpec((1, width), lambda k: (0, k)),
        ],
        out_specs=pl.BlockSpec((cycles, 128), lambda k: (0, 0)),
        scratch_shapes=[pltpu.VMEM((2, width // 128, 64, 128), F32), pltpu.VMEM((cycles, 128), F32)],
        name="synth",
    )(coeffs_t, tables, beam)


def iota(shape, dim):
    return lax.broadcasted_iota(jnp.int32, shape, dim)


def table_kernel(m_ref, out_ref):
    quarter = PIX // 4
    row = iota((32, 128), 0)
    mode, gain = [], []
    for s in range(2):
        m = jnp.zeros((32, 128), jnp.int32)
        for j in range(32):
            m = jnp.where(row == j, m_ref[2 * j + s], m)
        mode.append(m)
        gain.append(jnp.where(m == 0, 1.0, 2.0).astype(F32))
    lane = iota((32, 128), 1)

    def chunk(i, carry):
        first = i * 128
        for par in range(2):
            for s in range(2):
                k = (mode[s] * (2 * (lane + first) + par)) & (2 * PIX - 1)
                n = (k + quarter) >> 11
                angle = (k - (n << 11)).astype(F32) * F32(math.pi / PIX)
                sq = angle * angle
                c = -1 / 3628800
                for inv in (1 / 40320, -1 / 720, 1 / 24, -1 / 2, 1.0):
                    c = c * sq + F32(inv)
                d = 1 / 362880
                for inv in (-1 / 5040, 1 / 120, -1 / 6, 1.0):
                    d = d * sq + F32(inv)
                d = d * angle
                swap = (n & 1) == 1
                cosine = jnp.where(swap, d, c)
                sine = jnp.where(swap, c, d)
                cosine = jnp.where(((n + 1) & 2) == 2, -cosine, cosine)
                sine = jnp.where((n & 2) == 2, -sine, sine)
                for reim in range(2):
                    top = par * 128 + (2 * s + reim) * 32
                    for u in range(4):
                        turn = (mode[s] * u + reim) & 3
                        value = jnp.where((turn & 1) == 1, sine, cosine)
                        scale = jnp.where(((turn + 1) & 2) == 2, -gain[s], gain[s])
                        at = pl.ds(pl.multiple_of(u * quarter + first, 128), 128)
                        out_ref[top : top + 32, at] = (value * scale).astype(BF16)
        return carry

    lax.fori_loop(0, quarter // 128, chunk, 0)


def phase_table(m_values):
    return pl.pallas_call(
        table_kernel,
        out_shape=jax.ShapeDtypeStruct((256, PIX), BF16),
        in_specs=[pl.BlockSpec(memory_space=pltpu.SMEM)],
        out_specs=pl.BlockSpec(memory_space=pltpu.VMEM),
        cost_estimate=pl.CostEstimate(flops=8_000_000, bytes_accessed=2_097_152, transcendentals=0),
        name="phase_table",
    )(m_values)


def by_cycle(values, place):
    odd = jnp.zeros(place.shape, jnp.int32)
    for t in range(PER):
        odd = jnp.where(place == t, values[t], odd)
    return odd == 1


def pixel_kernel(ids_ref, x_ref, tab_ref, mix_ref, diag_ref, cross_ref, out_ref, rows_ref, acc_ref):
    fields = 2 * PAIRS
    parity = [ids_ref[t] & 1 for t in range(PER)]
    slot = iota((32, 128), 1) // 32
    rows_ref[...] = x_ref[...].astype(F32)
    per_cycle = [rows_ref[pl.ds(t, 32, stride=PER), :] for t in range(PER)]
    halves = []
    for high in range(2):
        blocks = []
        for sr in range(4):
            block = None
            for low in range(4):
                value = per_cycle[4 * high + low]
                shift = (low - sr) * 32 % 128
                value = pltpu.roll(value, shift, 1) if shift else value
                block = value if block is None else jnp.where(slot == low, value, block)
            blocks.append(block)
        halves.append(jnp.concatenate(blocks, 0))
    gathered = jnp.concatenate(halves, 1).astype(BF16)

    row, col = iota((fields * PER, 256), 0), iota((fields * PER, 256), 1)
    field = row // PER
    target = (row % PER) * 32 + field + jnp.where(field >= PAIRS, SLOT - PAIRS, 0)
    perm = jnp.where(col == target, 1.0, 0.0).astype(BF16)

    lhs = dot(perm, gathered, NT)
    odd_row = by_cycle(parity, iota(lhs.shape, 0) % PER)
    zero = jnp.zeros_like(lhs)
    lhs = jnp.concatenate(
        [jnp.where(odd_row, zero, lhs), jnp.where(odd_row, lhs, zero)], 1
    ).astype(BF16)

    width = 512
    for p in range(PIX // width):
        at = slice(p * width, (p + 1) * width)
        table = tab_ref[:, at]
        maps = dot(lhs, table, NN)
        mix = [mix_ref[0, c, :, at] for c in range(COMPS)]
        diag = [diag_ref[0, e, :, at] for e in range(2)]
        cross = cross_ref[0, :, at]
        back = [[None] * PAIRS, [None] * PAIRS]
        for chain in range(CHAINS):
            sky = []
            for e in range(2):
                total = None
                for c in range(COMPS):
                    f = e * PAIRS + chain * COMPS + c
                    part = maps[f * PER : (f + 1) * PER] * mix[c]
                    total = part if total is None else total + part
                sky.append(total)
            weighted = [
                diag[0] * sky[0] + cross * sky[1],
                cross * sky[0] + diag[1] * sky[1],
            ]
            for e in range(2):
                for c in range(COMPS):
                    back[e][chain * COMPS + c] = weighted[e] * mix[c]
        back = jnp.concatenate(back[0] + back[1], 0).astype(BF16)
        part = dot(table, back, NT)
        if p == 0:
            acc_ref[...] = part
        else:
            acc_ref[...] += part

    odd_lane = by_cycle(parity, iota((128, fields * PER), 1) % PER)
    returned = jnp.where(odd_lane, acc_ref[128:, :], acc_ref[:128, :]).astype(BF16)
    spread = dot(returned, perm, NN)
    for t in range(PER):
        high, low = divmod(t, 4)
        block = None
        for sr in range(4):
            value = spread[sr * 32 : (sr + 1) * 32, high * 128 : (high + 1) * 128]
            shift = (sr - low) * 32 % 128
            value = pltpu.roll(value, shift, 1) if shift else value
            block = value if block is None else jnp.where(slot == sr, value, block)
        rows_ref[pl.ds(t, 32, stride=PER), :] = block
    result = rows_ref[...].astype(BF16)
    out_ref[0] = result
    out_ref[1] = result


def pixels(cycle_ids, arrived, table, mixing, noise_diag, noise_cross):
    vmem = pl.BlockSpec(memory_space=pltpu.VMEM)
    return pl.pallas_call(
        pixel_kernel,
        out_shape=jax.ShapeDtypeStruct((2, 256, 128), BF16),
        in_specs=[pl.BlockSpec(memory_space=pltpu.SMEM)] + [vmem] * 5,
        out_specs=vmem,
        scratch_shapes=[pltpu.VMEM((256, 128), F32), pltpu.VMEM((256, 2 * PAIRS * PER), F32)],
        name="pixels",
    )(cycle_ids, arrived, table, mixing, noise_diag, noise_cross)


def adjoint_kernel(core_ref, r_ref, low_ref, high_ref, *rest):
    own_low, own_high, other_low, other_high, out_ref, lhs_ref, nat_ref = rest

    @pl.when(pl.program_id(0) == 0)
    def _():
        for b, index in enumerate((core_ref[0], 1 - core_ref[0])):
            turned = r_ref[index].astype(F32).T
            for s in range(2):
                rows = turned[s * 64 : (s + 1) * 64]
                slots = [rows[i * SLOT : (i + 1) * SLOT] for i in range(4)]
                at = slice(b * 64, (b + 1) * 64)
                lhs_ref[s, at, :256] = rows.astype(BF16)
                lhs_ref[s, at, 256:] = jnp.concatenate(crossed(slots), 0).astype(BF16)

    for half, tab_ref, own, other in (
        (0, low_ref, own_low, other_low),
        (1, high_ref, own_high, other_high),
    ):
        for s in range(2):
            sums = dot(lhs_ref[s, :, :256], tab_ref[s, 0], NN) + dot(
                lhs_ref[s, :, 256:], tab_ref[s, 1], NN
            )
            sums = sums[:64] * own[...] + sums[64:] * other[...]
            for i, place in enumerate(PLACE):
                nat_ref[half, s, pl.ds(place, SLOT, stride=4), :] = sums[i * SLOT : (i + 1) * SLOT]
            out_ref[half, 0, s] = nat_ref[half, s, :COLS, :].astype(BF16)


def adjoint(core, returned, tables, own_beam, other_beam):
    cycles = tables.shape[2]
    steps = 4

    def level(half):
        return lambda k, core: (0, 0, 0, 2 * (k + half * steps) + core[0])

    def beam_level(half):
        return lambda k, core: (0, 2 * (k + half * steps) + core[0])

    tab = [pl.BlockSpec((2, 2, cycles, 128), level(h)) for h in range(2)]
    beams = [pl.BlockSpec((1, 128), beam_level(h)) for h in range(2)]
    out = pl.pallas_call(
        adjoint_kernel,
        out_shape=jax.ShapeDtypeStruct((2, steps, 2, COLS, 128), BF16),
        grid_spec=pltpu.PrefetchScalarGridSpec(
            num_scalar_prefetch=1,
            grid=(steps,),
            in_specs=[pl.BlockSpec((2, cycles, 128), lambda k, core: (0, 0, 0))] + tab + beams * 2,
            out_specs=pl.BlockSpec((2, 1, 2, COLS, 128), lambda k, core: (0, k, 0, 0, 0)),
            scratch_shapes=[
                pltpu.VMEM((2, 128, 2 * cycles), BF16),
                pltpu.VMEM((2, 2, 64, 128), F32),
            ],
        ),
        name="adjoint",
    )(core, returned, tables, tables, own_beam, own_beam, other_beam, other_beam)
    return out.reshape(2 * steps, 2, COLS, 128)


def final_kernel(band_ref, sum_ref, coef_ref, prior_ref, out_ref):
    kind = iota((COLS, 128), 0) % (4 * COMPS) // 2
    prior = jnp.zeros((COLS, 128), F32)
    for k in range(2 * COMPS):
        prior = jnp.where(kind == k, prior_ref[k : k + 1, :], prior)
    for s in range(2):
        total = prior * coef_ref[s].astype(F32)
        for y in range(sum_ref.shape[0]):
            total = total + sum_ref[y, s].astype(F32)
        out_ref[s] = total


def final(band, gathered, coeffs_t, prior):
    return pl.pallas_call(
        final_kernel,
        out_shape=jax.ShapeDtypeStruct((2, COLS, 128), F32),
        grid_spec=pltpu.PrefetchScalarGridSpec(
            num_scalar_prefetch=1,
            grid=(1,),
            in_specs=[
                pl.BlockSpec(gathered.shape, lambda k, band: (0, 0, 0, 0)),
                pl.BlockSpec((2, COLS, 128), lambda k, band: (0, 0, band[0])),
                pl.BlockSpec((2 * COMPS, 128), lambda k, band: (0, 0)),
            ],
            out_specs=pl.BlockSpec((2, COLS, 128), lambda k, band: (0, 0, 0)),
        ),
        name="final",
    )(band, gathered, coeffs_t, prior)


def on_device(coeffs, tables, beam, mixing, noise_diag, noise_cross, prior, m_values, cycle_ids):
    core = lax.axis_index("core")
    band = (2 * lax.axis_index("y") + core).astype(jnp.int32)[None]
    core = core.astype(jnp.int32)[None]
    coeffs_t = coeffs.transpose(0, 2, 1)
    spectra = synth(coeffs_t, tables, beam)
    arrived = lax.all_to_all(spectra.reshape(32, PER, 128), "ma", 0, 0, tiled=True)
    table = phase_table(m_values)
    other_beam = lax.ppermute(beam, "core", [(0, 1), (1, 0)])
    returned = pixels(cycle_ids, arrived.reshape(256, 128), table, mixing, noise_diag, noise_cross)
    returned = lax.all_to_all(
        returned.reshape(64, PER, 128), ("core", "ma"), 0, 0, tiled=True
    ).reshape(2, 256, 128)
    partial = adjoint(core, returned, tables, beam, other_beam)
    gathered = lax.all_to_all(partial, "y", 0, 0, tiled=True)
    return final(band, gathered, coeffs_t, prior).transpose(0, 2, 1)


def solution(mesh):
    bands, modes = mesh.devices.shape
    fine = Mesh(mesh.devices.reshape(bands // 2, 2, modes), ("y", "core", "ma"))
    band = ("y", "core")
    in_specs = (
        P("ma", None, None),
        P("ma", None, None, None),
        P(band, None),
        P(band, None, "ma", None),
        P(band, None, "ma", None),
        P(band, "ma", None),
        P(None, band),
        P(),
        P("ma"),
    )
    return jax.shard_map(
        on_device, mesh=fine, in_specs=in_specs, out_specs=P("ma", band, None), check_vma=False
    )
```

time: 147 us -> 74.9 us (0.51)
  waiting for transfers between devices: 55.3 us -> 23.9 us
  other arithmetic: 20.2 us -> 0 us
  Pallas kernels: 0 us -> 19.2 us
  blocking collectives: 17.8 us -> 0 us
  starting transfers between devices: 13.7 us -> 29.1 us
  matrix products: 14.9 us -> 0 us
  between operations: 13.8 us -> 0.05 us
  local copies, waits for them, and re-layouts: 9.93 us -> 1.95 us
    reduce_scatter x1 -> x0, waiting for transfers between devices: 55.2 us -> none  [on_device(): lax.psum_scatter(partial_sum, 'band', scatter_dimension=1, tiled=True)]
    all_to_all x1 -> x3, waiting for transfers between devices: 0.01 us -> 23.1 us  [the longest x1 10.9 us: on_device(): gathered = lax.all_to_all(partial, 'y', 0, 0, tiled=True)]
    pallas_call x0 -> x5, Pallas kernels: none -> 19.2 us  [the longest x1 4.7 us: synth(): pl.pallas_call(synth_kernel, out_shape=jax.ShapeDtypeStruct((cycles, 128)...]
    all_to_all x1 -> x0, blocking collectives: 17.8 us -> none  [on_device(): lax.all_to_all(returned, 'ma', split_axis=0, concat_axis=1, tiled=True)]
    dot_general x5 -> x0, matrix products: 14.9 us -> none  [the longest x1 3.94 us: on_device(): jnp.einsum('rfp,rjp->rfj', returned_map, cycle_tables, preferred_element_...]
    all_to_all x1 -> x3, starting transfers between devices: 13.7 us -> 26.9 us  [the longest x1 13.7 us: on_device(): lax.all_to_all(spectra.reshape(32, PER, 128), 'ma', 0, 0, tiled=True)]
    another operation x5 -> x0, other arithmetic: 10.4 us -> none
    reshape x9 -> x0, local copies, waits for them, and re-layouts: 5.02 us -> none  [the longest x1 3.88 us: on_device(): pixel_maps.reshape(cycle_count, fields // (2 * COMPS), COMPS, 2, PIX)]
  transfers between devices with their start and end apart: 2 -> 4, of which waited for: 1 -> 4; matrix products, arithmetic and copies ran while one was open for 7% -> 0% of each run, Pallas kernels for 0% -> 5%
where the time goes in v1:
time: 74.9 us; the launch traced here: 74.3 us
  starting transfers between devices  29.1 us (39%)
  waiting for transfers between devices  23.9 us (32%)
  Pallas kernels  19.2 us (26%)
  local copies, waits for them, and re-layouts  1.95 us (3%)
    all_to_all x1, starting transfers between devices, on_device(): lax.all_to_all(spectra.reshape(32, PER, 128), 'ma', 0, 0, tiled=True)  13.7 us
    all_to_all x1, waiting for transfers between devices, on_device(): gathered = lax.all_to_all(partial, 'y', 0, 0, tiled=True)  10.9 us
    all_to_all x1, waiting for transfers between devices, on_device(): lax.all_to_all(returned.reshape(64, PER, 128), ('core', 'ma'), 0, 0, tile...  7.38 us
    all_to_all x1, starting transfers between devices, on_device(): gathered = lax.all_to_all(partial, 'y', 0, 0, tiled=True)  6.82 us
    all_to_all x1, starting transfers between devices, on_device(): lax.all_to_all(returned.reshape(64, PER, 128), ('core', 'ma'), 0, 0, tile...  6.36 us
    all_to_all x1, waiting for transfers between devices, on_device(): lax.all_to_all(spectra.reshape(32, PER, 128), 'ma', 0, 0, tiled=True)  4.82 us
    pallas_call x1, Pallas kernels, synth(): pl.pallas_call(synth_kernel, out_shape=jax.ShapeDtypeStruct((cycles, 128)...  4.7 us
    pallas_call x1, Pallas kernels, pixels(): pl.pallas_call(pixel_kernel, out_shape=jax.ShapeDtypeStruct((2, 256, 128)...  4.61 us
  transfers between devices with their start and end apart: 4, of which 4 were waited for; matrix products, arithmetic and copies ran while one was open for 0% of the time, Pallas kernels for 5%

profile of v1, /device:TPU:1, one launch (start us, length us, event | category | flops | bytes accessed | tf_op | source)
XLA Modules:
  0.0 74.3 jit_solution(8129137929702361753)
XLA Ops:
  0.0 0.0 copy-start.3
  0.0 4.7 %synth.1 = bf16[256,128]{1,0:T(8,128)(2,1)} custom-call(bf16[2,48,2048]{2,1,0:T(8,128)(2,1)} %bitcast.9, bf16[2,2,256,2048]{3,2,1,0:T(8,128)(2,1)} %high_ref.1, f32[1,2048]{1,0:T(1,128)} %rest_1_.1), custom_call_target="tpu_custom_call" | custom-call | tf_op jit(solution)/shard_map/synth/pallas_call | solution.py:76
  4.7 13.7 %all-to-all-start = ((bf16[32,8,128]{2,1,0:T(8,128)(2,1)}), bf16[32,8,128]{2,1,0:T(8,128)(2,1)S(1)}, u32[]{:S(2)}, u32[]{:S(2)}) async-start(bf16[32,8,128]{2,1,0:T(8,128)(2,1)} %bitcast.14), calls=%async_computation | async-start | bytes 131072 | tf_op jit(solution)/shard_map/all_to_all | solution.py:345
  18.4 4.0 %phase_table.1.tab_ref = bf16[256,4096]{1,0:T(8,128)(2,1)} custom-call(s32[64]{0:T(128)} %m_ref.1), custom_call_target="tpu_custom_call" | custom-call | flops 8000000 | bytes 2097152 | tf_op jit(solution)/shard_map/phase_table/pallas_call | solution.py:141
  22.4 4.8 %all-to-all-done = bf16[32,8,128]{2,1,0:T(8,128)(2,1)S(1)} async-done(((bf16[32,8,128]{2,1,0:T(8,128)(2,1)}), bf16[32,8,128]{2,1,0:T(8,128)(2,1)S(1)}, u32[]{:S(2)}, u32[]{:S(2)}) %all-to-all-start) | async-done | bytes 65568 | tf_op jit(solution)/shard_map/all_to_all | solution.py:345
  27.2 0.0 copy-start.2
  27.2 0.6 copy-done.2
  27.9 4.6 %pixels.1 = bf16[2,256,128]{2,1,0:T(8,128)(2,1)} custom-call(s32[8]{0:T(128)} %ids_ref.1, bf16[256,128]{1,0:T(8,128)(2,1)} %bitcast.15, bf16[256,4096]{1,0:T(8,128)(2,1)} %phase_table.1.tab_ref, f32[1,3,8,4096]{3,2,1,0:T(8,128)} %mix_ref.1, f32[1,2,8,4096]{3,2,1,0:T(8,128)} %diag_ref.1, f32[1,8,4096]{2,1,0:T(8,128)} %cross_ref.1), custom_call_target="tpu_custom_call" | custom-call | tf_op jit(solution)/shard_map/pixels/pallas_call | solution.py:241
  32.5 6.4 %all-to-all-start.1 = ((bf16[64,8,128]{2,1,0:T(8,128)(2,1)}), bf16[64,8,128]{2,1,0:T(8,128)(2,1)S(1)}, u32[]{:S(2)}, u32[]{:S(2)}) async-start(bf16[64,8,128]{2,1,0:T(8,128)(2,1)} %bitcast.13), calls=%async_computation.1 | async-start | bytes 262144 | tf_op jit(solution)/shard_map/all_to_all | solution.py:349
  38.8 0.0 copy-done.3
  38.8 2.3 %collective-permute-start = (f32[1,2048]{1,0:T(1,128)S(1)}, f32[1,2048]{1,0:T(1,128)S(1)}, u32[]{:S(2)}, u32[]{:S(2)}) collective-permute-start(f32[1,2048]{1,0:T(1,128)S(1)} %copy-done.3), channel_id=1, source_target_pairs={{0,32},{32,0},{1,33},{33,1},{2,34},{34,2},{3,35},{35,3},{4,36},{36... | collective-permute-start | bytes 24584 | tf_op jit(solution)/shard_map/ppermute | solution.py:347
  41.1 0.8 %collective-permute-done.rest_2_.rest_3_ = f32[1,2048]{1,0:T(1,128)S(1)} collective-permute-done((f32[1,2048]{1,0:T(1,128)S(1)}, f32[1,2048]{1,0:T(1,128)S(1)}, u32[]{:S(2)}, u32[]{:S(2)}) %collective-permute-start) | collective-permute-done | bytes 8224 | tf_op jit(solution)/shard_map/ppermute | solution.py:347
  41.9 0.0 copy-start.4
  41.9 7.4 %all-to-all-done.1 = bf16[64,8,128]{2,1,0:T(8,128)(2,1)S(1)} async-done(((bf16[64,8,128]{2,1,0:T(8,128)(2,1)}), bf16[64,8,128]{2,1,0:T(8,128)(2,1)S(1)}, u32[]{:S(2)}, u32[]{:S(2)}) %all-to-all-start.1) | async-done | bytes 131104 | tf_op jit(solution)/shard_map/all_to_all | solution.py:349
  49.3 0.0 copy-start.1
  49.3 0.0 copy-done.4
  49.3 0.6 copy-done.1
  50.0 4.3 %adjoint.1 = bf16[2,4,2,48,128]{4,3,2,1,0:T(8,128)(2,1)} custom-call(s32[1]{0:T(128)} %bitcast.1.core_ref, bf16[2,256,128]{2,1,0:T(8,128)(2,1)} %bitcast.12, bf16[2,2,256,2048]{3,2,1,0:T(8,128)(2,1)} %high_ref.1, bf16[2,2,256,2048]{3,2,1,0:T(8,128)(2,1)} %high_ref.1, f32[1,2048]{1,0:T(1,128)} %rest_1_.1, f32[1,2048]{1,0:T(1,128)} %rest_1_.1, ...), custom_call_target="tpu_custom_call" | custom-call | tf_op jit(solution)/shard_map/adjoint/pallas_call | solution.py:291
  54.3 6.8 %all-to-all-start.2 = ((bf16[8,2,48,128]{3,2,1,0:T(8,128)(2,1)}), bf16[8,2,48,128]{3,2,1,0:T(8,128)(2,1)S(1)}, u32[]{:S(2)}, u32[]{:S(2)}) async-start(bf16[8,2,48,128]{3,2,1,0:T(8,128)(2,1)} %bitcast.11), calls=%async_computation.2 | async-start | bytes 393216 | tf_op jit(solution)/shard_map/all_to_all | solution.py:353
  61.1 10.9 %all-to-all-done.2.sum_ref = bf16[8,2,48,128]{3,2,1,0:T(8,128)(2,1)S(1)} async-done(((bf16[8,2,48,128]{3,2,1,0:T(8,128)(2,1)}), bf16[8,2,48,128]{3,2,1,0:T(8,128)(2,1)S(1)}, u32[]{:S(2)}, u32[]{:S(2)}) %all-to-all-start.2) | async-done | bytes 196640 | tf_op jit(solution)/shard_map/all_to_all | solution.py:353
  72.0 0.0 copy-start
  72.0 0.7 copy-done
  72.7 1.6 %final.1 = f32[2,48,128]{2,1,0:T(8,128)} custom-call(s32[1]{0:T(128)} %bitcast.band_ref, bf16[8,2,48,128]{3,2,1,0:T(8,128)(2,1)} %copy-done, bf16[2,48,2048]{2,1,0:T(8,128)(2,1)} %bitcast.10, f32[6,128]{1,0:T(8,128)} %prior_ref.1), custom_call_target="tpu_custom_call" | custom-call | tf_op jit(solution)/shard_map/final/pallas_call | solution.py:322
Async XLA Ops:
  0.0 38.8 %copy-start.3 = (f32[1,2048]{1,0:T(1,128)S(1)}, f32[1,2048]{1,0:T(1,128)}, u32[]{:S(2)}) copy-start(f32[1,2048]{1,0:T(1,128)} %rest_1_.1) | copy-start | bytes 24580
  4.7 22.5 %all-to-all-start = ((bf16[32,8,128]{2,1,0:T(8,128)(2,1)}), bf16[32,8,128]{2,1,0:T(8,128)(2,1)S(1)}, u32[]{:S(2)}, u32[]{:S(2)}) async-start(bf16[32,8,128]{2,1,0:T(8,128)(2,1)} %bitcast.14), calls=%async_computation | async-start | bytes 131072 | tf_op jit(solution)/shard_map/all_to_all | solution.py:345
  27.2 0.6 copy-start.2
  32.5 16.8 %all-to-all-start.1 = ((bf16[64,8,128]{2,1,0:T(8,128)(2,1)}), bf16[64,8,128]{2,1,0:T(8,128)(2,1)S(1)}, u32[]{:S(2)}, u32[]{:S(2)}) async-start(bf16[64,8,128]{2,1,0:T(8,128)(2,1)} %bitcast.13), calls=%async_computation.1 | async-start | bytes 262144 | tf_op jit(solution)/shard_map/all_to_all | solution.py:349
  38.8 3.1 %collective-permute-start = (f32[1,2048]{1,0:T(1,128)S(1)}, f32[1,2048]{1,0:T(1,128)S(1)}, u32[]{:S(2)}, u32[]{:S(2)}) collective-permute-start(f32[1,2048]{1,0:T(1,128)S(1)} %copy-done.3), channel_id=1, source_target_pairs={{0,32},{32,0},{1,33},{33,1},{2,34},{34,2},{3,35},{35,3},{4,36},{36... | collective-permute-start | bytes 24584 | tf_op jit(solution)/shard_map/ppermute | solution.py:347
  41.9 7.4 %copy-start.4 = (f32[1,2048]{1,0:T(1,128)}, f32[1,2048]{1,0:T(1,128)S(1)}, u32[]{:S(2)}) copy-start(f32[1,2048]{1,0:T(1,128)S(1)} %collective-permute-done.rest_2_.rest_3_) | copy-start | bytes 24580
  49.3 0.7 copy-start.1
  54.3 17.8 %all-to-all-start.2 = ((bf16[8,2,48,128]{3,2,1,0:T(8,128)(2,1)}), bf16[8,2,48,128]{3,2,1,0:T(8,128)(2,1)S(1)}, u32[]{:S(2)}, u32[]{:S(2)}) async-start(bf16[8,2,48,128]{3,2,1,0:T(8,128)(2,1)} %bitcast.11), calls=%async_computation.2 | async-start | bytes 393216 | tf_op jit(solution)/shard_map/all_to_all | solution.py:353
  72.0 0.7 copy-start

commit v2 on v1

--- a/solution.py
+++ b/solution.py
@@ -24,6 +24,10 @@
 NN = (((1,), (0,)), ((), ()))
 
 
+def grant(mib):
+    return pltpu.CompilerParams(vmem_limit_bytes=mib << 20)
+
+
 def dot(a, b, dims):
     return lax.dot_general(a, b, dims, preferred_element_type=F32)
 
@@ -32,58 +36,64 @@
     return [-slots[3], slots[2], slots[1], -slots[0]]
 
 
-def synth_kernel(coef_ref, tab_ref, beam_ref, out_ref, nat_ref, acc_ref):
-    step = pl.program_id(0)
-
-    @pl.when(step == 0)
-    def _():
-        nat_ref[...] = jnp.zeros_like(nat_ref)
-
-    total = None
+CHUNKS = 4
+
+
+def synth_kernel(coef_hbm, tab_hbm, beam_hbm, out_ref, coef_ref, tab_ref, beam_ref, nat_ref, rows_ref, sems):
+    levels = coef_ref.shape[2]
+    width = levels // CHUNKS
+    heads = [
+        pltpu.make_async_copy(beam_hbm, beam_ref, sems.at[CHUNKS]),
+        pltpu.make_async_copy(coef_hbm, coef_ref, sems.at[CHUNKS + 1]),
+    ]
+    for head in heads:
+        head.start()
+    copies = []
+    for c in range(CHUNKS):
+        at = pl.ds(c * width, width)
+        copies.append(pltpu.make_async_copy(tab_hbm.at[:, :, :, at], tab_ref.at[c], sems.at[c]))
+        copies[-1].start()
+    nat_ref[...] = jnp.zeros_like(nat_ref)
+    for head in heads:
+        head.wait()
     for s in range(2):
-        beamed = (coef_ref[s].astype(F32) * beam_ref[...]).astype(BF16)
-        tiles = range(beamed.shape[1] // 128)
-        for j in tiles:
-            nat_ref[s, j, :COLS, :] = beamed[:, j * 128 : (j + 1) * 128].astype(F32)
-        slots = [
-            jnp.concatenate([nat_ref[s, j, pl.ds(p, SLOT, stride=4), :] for j in tiles], 1)
-            for p in PLACE
-        ]
-        none = jnp.zeros((4 * SLOT, beamed.shape[1]), BF16)
-        for which, rows in enumerate((slots, crossed(slots))):
-            rows = jnp.concatenate(rows, 0).astype(BF16)
-            rows = jnp.concatenate([rows, none] if s == 0 else [none, rows], 0)
-            part = dot(tab_ref[s, which], rows, NT)
-            total = part if total is None else total + part
-
-    @pl.when(step == 0)
-    def _():
-        acc_ref[...] = total
-
-    @pl.when(step > 0)
-    def _():
-        acc_ref[...] += total
-
-    @pl.when(step == pl.num_programs(0) - 1)
-    def _():
-        out_ref[...] = acc_ref[...].astype(BF16)
-
-
-def synth(coeffs_t, tables, beam, chunks=4):
+        for j in range(levels // 128):
+            at = slice(j * 128, (j + 1) * 128)
+            beamed = (coef_ref[s, :, at].astype(F32) * beam_ref[:, at]).astype(BF16)
+            nat_ref[s, j, :COLS, :] = beamed.astype(F32)
+            slots = [nat_ref[s, j, pl.ds(p, SLOT, stride=4), :] for p in PLACE]
+            for which, rows in enumerate((slots, crossed(slots))):
+                rows_ref[s, which, :, at] = jnp.concatenate(rows, 0).astype(BF16)
+    total = [None, None]
+    for c in range(CHUNKS):
+        copies[c].wait()
+        for s in range(2):
+            for which in range(2):
+                rows = rows_ref[s, which, :, c * width : (c + 1) * width]
+                part = dot(tab_ref[c, s, which], rows, NT)
+                total[s] = part if total[s] is None else total[s] + part
+    out_ref[...] = jnp.concatenate(total, 1).astype(BF16)
+
+
+def synth(coeffs_t, tables, beam):
     _, cols, levels = coeffs_t.shape
     cycles = tables.shape[2]
-    width = levels // chunks
+    hbm = pl.BlockSpec(memory_space=pltpu.HBM)
+    vmem = pl.BlockSpec(memory_space=pltpu.VMEM)
     return pl.pallas_call(
         synth_kernel,
         out_shape=jax.ShapeDtypeStruct((cycles, 128), BF16),
-        grid=(chunks,),
-        in_specs=[
-            pl.BlockSpec((2, cols, width), lambda k: (0, 0, k)),
-            pl.BlockSpec((2, 2, cycles, width), lambda k: (0, 0, 0, k)),
-            pl.BlockSpec((1, width), lambda k: (0, k)),
+        in_specs=[hbm] * 3,
+        out_specs=vmem,
+        scratch_shapes=[
+            pltpu.VMEM((2, cols, levels), BF16),
+            pltpu.VMEM((CHUNKS, 2, 2, cycles, levels // CHUNKS), BF16),
+            pltpu.VMEM((1, levels), F32),
+            pltpu.VMEM((2, levels // 128, 4 * SLOT, 128), F32),
+            pltpu.VMEM((2, 2, 4 * SLOT, levels), BF16),
+            pltpu.SemaphoreType.DMA((CHUNKS + 2,)),
         ],
-        out_specs=pl.BlockSpec((cycles, 128), lambda k: (0, 0)),
-        scratch_shapes=[pltpu.VMEM((2, width // 128, 64, 128), F32), pltpu.VMEM((cycles, 128), F32)],
+        compiler_params=grant(12),
         name="synth",
     )(coeffs_t, tables, beam)
 
@@ -144,6 +154,7 @@
         in_specs=[pl.BlockSpec(memory_space=pltpu.SMEM)],
         out_specs=pl.BlockSpec(memory_space=pltpu.VMEM),
         cost_estimate=pl.CostEstimate(flops=8_000_000, bytes_accessed=2_097_152, transcendentals=0),
+        compiler_params=grant(6),
         name="phase_table",
     )(m_values)
 
@@ -187,7 +198,7 @@
         [jnp.where(odd_row, zero, lhs), jnp.where(odd_row, lhs, zero)], 1
     ).astype(BF16)
 
-    width = 512
+    width = 2048
     for p in range(PIX // width):
         at = slice(p * width, (p + 1) * width)
         table = tab_ref[:, at]
@@ -244,66 +255,94 @@
         in_specs=[pl.BlockSpec(memory_space=pltpu.SMEM)] + [vmem] * 5,
         out_specs=vmem,
         scratch_shapes=[pltpu.VMEM((256, 128), F32), pltpu.VMEM((256, 2 * PAIRS * PER), F32)],
+        compiler_params=grant(10),
         name="pixels",
     )(cycle_ids, arrived, table, mixing, noise_diag, noise_cross)
 
 
-def adjoint_kernel(core_ref, r_ref, low_ref, high_ref, *rest):
-    own_low, own_high, other_low, other_high, out_ref, lhs_ref, nat_ref = rest
-
-    @pl.when(pl.program_id(0) == 0)
-    def _():
-        for b, index in enumerate((core_ref[0], 1 - core_ref[0])):
-            turned = r_ref[index].astype(F32).T
-            for s in range(2):
-                rows = turned[s * 64 : (s + 1) * 64]
-                slots = [rows[i * SLOT : (i + 1) * SLOT] for i in range(4)]
-                at = slice(b * 64, (b + 1) * 64)
-                lhs_ref[s, at, :256] = rows.astype(BF16)
-                lhs_ref[s, at, 256:] = jnp.concatenate(crossed(slots), 0).astype(BF16)
-
-    for half, tab_ref, own, other in (
-        (0, low_ref, own_low, other_low),
-        (1, high_ref, own_high, other_high),
-    ):
+def fetch_kernel(core_ref, tab_hbm, beam_ref, out_ref, own_ref, sent_ref, sems):
+    blocks = tab_hbm.shape[3] // 256
+    copies = []
+    for k in range(blocks):
+        source = pl.ds(pl.multiple_of(256 * k + 128 * core_ref[0], 128), 128)
+        place = pl.ds(128 * k, 128)
+        copies.append(
+            pltpu.make_async_copy(
+                tab_hbm.at[:, :, :, source], out_ref.at[:, :, :, place], sems.at[k]
+            )
+        )
+        copies[-1].start()
+        pair = [beam_ref[:, (2 * k + c) * 128 : (2 * k + c + 1) * 128] for c in range(2)]
+        second = core_ref[0] == 1
+        own_ref[:, 128 * k : 128 * (k + 1)] = jnp.where(second, pair[1], pair[0])
+        sent_ref[:, 128 * k : 128 * (k + 1)] = jnp.where(second, pair[0], pair[1])
+    for copy in copies:
+        copy.wait()
+
+
+def fetch(core, tables, beam):
+    levels = tables.shape[3]
+    hbm = pl.BlockSpec(memory_space=pltpu.HBM)
+    vmem = pl.BlockSpec(memory_space=pltpu.VMEM)
+    return pl.pallas_call(
+        fetch_kernel,
+        out_shape=(
+            jax.ShapeDtypeStruct(tables.shape[:3] + (levels // 2,), BF16),
+            jax.ShapeDtypeStruct((1, levels // 2), F32),
+            jax.ShapeDtypeStruct((1, levels // 2), F32),
+        ),
+        in_specs=[pl.BlockSpec(memory_space=pltpu.SMEM), hbm, vmem],
+        out_specs=(vmem, vmem, vmem),
+        scratch_shapes=[pltpu.SemaphoreType.DMA((levels // 256,))],
+        compiler_params=grant(4),
+        cost_estimate=pl.CostEstimate(flops=0, bytes_accessed=4_194_304, transcendentals=0),
+        name="fetch",
+    )(core, tables, beam)
+
+
+def adjoint_kernel(core_ref, r_ref, tab_ref, own_ref, other_ref, out_ref, lhs_ref, nat_ref):
+    cycles = tab_ref.shape[2]
+    for b, index in enumerate((core_ref[0], 1 - core_ref[0])):
+        turned = r_ref[index].astype(F32).T
         for s in range(2):
-            sums = dot(lhs_ref[s, :, :256], tab_ref[s, 0], NN) + dot(
-                lhs_ref[s, :, 256:], tab_ref[s, 1], NN
+            rows = turned[s * 64 : (s + 1) * 64]
+            slots = [rows[i * SLOT : (i + 1) * SLOT] for i in range(4)]
+            at = slice(b * 64, (b + 1) * 64)
+            lhs_ref[s, 0, at, :] = rows.astype(BF16)
+            lhs_ref[s, 1, at, :] = jnp.concatenate(crossed(slots), 0).astype(BF16)
+
+    width = 256
+    for s in range(2):
+        for k in range(tab_ref.shape[3] // width):
+            at = slice(k * width, (k + 1) * width)
+            sums = dot(lhs_ref[s, 0], tab_ref[s, 0, :, at], NN) + dot(
+                lhs_ref[s, 1], tab_ref[s, 1, :, at], NN
             )
-            sums = sums[:64] * own[...] + sums[64:] * other[...]
-            for i, place in enumerate(PLACE):
-                nat_ref[half, s, pl.ds(place, SLOT, stride=4), :] = sums[i * SLOT : (i + 1) * SLOT]
-            out_ref[half, 0, s] = nat_ref[half, s, :COLS, :].astype(BF16)
+            sums = sums[:64] * own_ref[:, at] + sums[64:] * other_ref[:, at]
+            for h in range(width // 128):
+                y = k * (width // 128) + h
+                for i, place in enumerate(PLACE):
+                    part = sums[i * SLOT : (i + 1) * SLOT, h * 128 : (h + 1) * 128]
+                    nat_ref[s, y, pl.ds(place, SLOT, stride=4), :] = part
+                out_ref[y, s] = nat_ref[s, y, :COLS, :].astype(BF16)
 
 
 def adjoint(core, returned, tables, own_beam, other_beam):
-    cycles = tables.shape[2]
-    steps = 4
-
-    def level(half):
-        return lambda k, core: (0, 0, 0, 2 * (k + half * steps) + core[0])
-
-    def beam_level(half):
-        return lambda k, core: (0, 2 * (k + half * steps) + core[0])
-
-    tab = [pl.BlockSpec((2, 2, cycles, 128), level(h)) for h in range(2)]
-    beams = [pl.BlockSpec((1, 128), beam_level(h)) for h in range(2)]
-    out = pl.pallas_call(
+    cycles, levels = tables.shape[2:]
+    blocks = levels // 128
+    vmem = pl.BlockSpec(memory_space=pltpu.VMEM)
+    return pl.pallas_call(
         adjoint_kernel,
-        out_shape=jax.ShapeDtypeStruct((2, steps, 2, COLS, 128), BF16),
-        grid_spec=pltpu.PrefetchScalarGridSpec(
-            num_scalar_prefetch=1,
-            grid=(steps,),
-            in_specs=[pl.BlockSpec((2, cycles, 128), lambda k, core: (0, 0, 0))] + tab + beams * 2,
-            out_specs=pl.BlockSpec((2, 1, 2, COLS, 128), lambda k, core: (0, k, 0, 0, 0)),
-            scratch_shapes=[
-                pltpu.VMEM((2, 128, 2 * cycles), BF16),
-                pltpu.VMEM((2, 2, 64, 128), F32),
-            ],
-        ),
+        out_shape=jax.ShapeDtypeStruct((blocks, 2, COLS, 128), BF16),
+        in_specs=[pl.BlockSpec(memory_space=pltpu.SMEM)] + [vmem] * 4,
+        out_specs=vmem,
+        scratch_shapes=[
+            pltpu.VMEM((2, 2, 128, cycles), BF16),
+            pltpu.VMEM((2, blocks, 64, 128), F32),
+        ],
+        compiler_params=grant(8),
         name="adjoint",
-    )(core, returned, tables, tables, own_beam, own_beam, other_beam, other_beam)
-    return out.reshape(2 * steps, 2, COLS, 128)
+    )(core, returned, tables, own_beam, other_beam)
 
 
 def final_kernel(band_ref, sum_ref, coef_ref, prior_ref, out_ref):
@@ -311,27 +350,22 @@
     prior = jnp.zeros((COLS, 128), F32)
     for k in range(2 * COMPS):
         prior = jnp.where(kind == k, prior_ref[k : k + 1, :], prior)
+    at = pl.ds(pl.multiple_of(128 * band_ref[0], 128), 128)
     for s in range(2):
-        total = prior * coef_ref[s].astype(F32)
+        total = prior * coef_ref[s, :, at].astype(F32)
         for y in range(sum_ref.shape[0]):
             total = total + sum_ref[y, s].astype(F32)
         out_ref[s] = total
 
 
 def final(band, gathered, coeffs_t, prior):
+    vmem = pl.BlockSpec(memory_space=pltpu.VMEM)
     return pl.pallas_call(
         final_kernel,
         out_shape=jax.ShapeDtypeStruct((2, COLS, 128), F32),
-        grid_spec=pltpu.PrefetchScalarGridSpec(
-            num_scalar_prefetch=1,
-            grid=(1,),
-            in_specs=[
-                pl.BlockSpec(gathered.shape, lambda k, band: (0, 0, 0, 0)),
-                pl.BlockSpec((2, COLS, 128), lambda k, band: (0, 0, band[0])),
-                pl.BlockSpec((2 * COMPS, 128), lambda k, band: (0, 0)),
-            ],
-            out_specs=pl.BlockSpec((2, COLS, 128), lambda k, band: (0, 0, 0)),
-        ),
+        in_specs=[pl.BlockSpec(memory_space=pltpu.SMEM)] + [vmem] * 3,
+        out_specs=vmem,
+        compiler_params=grant(4),
         name="final",
     )(band, gathered, coeffs_t, prior)
 
@@ -341,15 +375,21 @@
     band = (2 * lax.axis_index("y") + core).astype(jnp.int32)[None]
     core = core.astype(jnp.int32)[None]
     coeffs_t = coeffs.transpose(0, 2, 1)
-    spectra = synth(coeffs_t, tables, beam)
+    stored = pltpu.with_memory_space_constraint(tables, pltpu.HBM)
+    spectra = synth(
+        pltpu.with_memory_space_constraint(coeffs_t, pltpu.HBM),
+        stored,
+        pltpu.with_memory_space_constraint(beam, pltpu.HBM),
+    )
     arrived = lax.all_to_all(spectra.reshape(32, PER, 128), "ma", 0, 0, tiled=True)
     table = phase_table(m_values)
-    other_beam = lax.ppermute(beam, "core", [(0, 1), (1, 0)])
     returned = pixels(cycle_ids, arrived.reshape(256, 128), table, mixing, noise_diag, noise_cross)
     returned = lax.all_to_all(
         returned.reshape(64, PER, 128), ("core", "ma"), 0, 0, tiled=True
     ).reshape(2, 256, 128)
-    partial = adjoint(core, returned, tables, beam, other_beam)
+    level_tables, own_beam, sent_beam = fetch(core, stored, beam)
+    other_beam = lax.ppermute(sent_beam, "core", [(0, 1), (1, 0)])
+    partial = adjoint(core, returned, level_tables, own_beam, other_beam)
     gathered = lax.all_to_all(partial, "y", 0, 0, tiled=True)
     return final(band, gathered, coeffs_t, prior).transpose(0, 2, 1)
 

time: 74.9 us -> 66 us (0.88)
  Pallas kernels: 19.2 us -> 12.5 us
  local copies, waits for them, and re-layouts: 1.95 us -> 0.05 us
    unnamed x10 -> x16, local copies, waits for them, and re-layouts: 1.95 us -> 0.05 us
    all_to_all x1, waiting for transfers between devices: 7.38 us -> 5.58 us  [on_device(): lax.all_to_all(returned.reshape(64, PER, 128), ('core', 'ma'), 0, 0, tile...]
    pallas_call x1, Pallas kernels: 4.61 us -> 2.89 us  [pixels(): pl.pallas_call(pixel_kernel, out_shape=jax.ShapeDtypeStruct((2, 256, 128)...]
    pallas_call x1, Pallas kernels: 4 us -> 2.52 us  [phase_table(): pl.pallas_call(table_kernel, out_shape=jax.ShapeDtypeStruct((256, PIX), B...]
    all_to_all x1, waiting for transfers between devices: 4.82 us -> 6.27 us  [on_device(): lax.all_to_all(spectra.reshape(32, PER, 128), 'ma', 0, 0, tiled=True)]
    pallas_call x1 -> x2, Pallas kernels: 4.3 us -> 2.86 us  [the longest x1 1.64 us: fetch(): pl.pallas_call(fetch_kernel, out_shape=(jax.ShapeDtypeStruct(tables.shape...]
    pallas_call x1, Pallas kernels: 4.7 us -> 3.5 us  [synth(): pl.pallas_call(synth_kernel, out_shape=jax.ShapeDtypeStruct((cycles, 128)...]
    pallas_call x1, Pallas kernels: 1.64 us -> 0.69 us  [final(): pl.pallas_call(final_kernel, out_shape=jax.ShapeDtypeStruct((2, COLS, 128...]
  transfers between devices with their start and end apart: 4 -> 4, of which waited for: 4 -> 4; matrix products, arithmetic and copies ran while one was open for 0% -> 0% of each run, Pallas kernels for 5% -> 6%
where the time goes in v2:
time: 66 us; the launch traced here: 65.7 us
  starting transfers between devices  29.4 us (45%)
  waiting for transfers between devices  23.6 us (36%)
  Pallas kernels  12.5 us (19%)
    all_to_all x1, starting transfers between devices, on_device(): lax.all_to_all(spectra.reshape(32, PER, 128), 'ma', 0, 0, tiled=True)  13.8 us
    all_to_all x1, waiting for transfers between devices, on_device(): gathered = lax.all_to_all(partial, 'y', 0, 0, tiled=True)  10.9 us
    all_to_all x1, starting transfers between devices, on_device(): gathered = lax.all_to_all(partial, 'y', 0, 0, tiled=True)  6.82 us
    all_to_all x1, starting transfers between devices, on_device(): lax.all_to_all(returned.reshape(64, PER, 128), ('core', 'ma'), 0, 0, tile...  6.35 us
    all_to_all x1, waiting for transfers between devices, on_device(): lax.all_to_all(spectra.reshape(32, PER, 128), 'ma', 0, 0, tiled=True)  6.27 us
    all_to_all x1, waiting for transfers between devices, on_device(): lax.all_to_all(returned.reshape(64, PER, 128), ('core', 'ma'), 0, 0, tile...  5.58 us
    pallas_call x1, Pallas kernels, synth(): pl.pallas_call(synth_kernel, out_shape=jax.ShapeDtypeStruct((cycles, 128)...  3.5 us
    pallas_call x1, Pallas kernels, pixels(): pl.pallas_call(pixel_kernel, out_shape=jax.ShapeDtypeStruct((2, 256, 128)...  2.89 us
  transfers between devices with their start and end apart: 4, of which 4 were waited for; matrix products, arithmetic and copies ran while one was open for 0% of the time, Pallas kernels for 6%

profile of v2, /device:TPU:1, one launch (start us, length us, event | category | flops | bytes accessed | tf_op | source)
XLA Modules:
  0.0 65.7 jit_solution(4632636121212510938)
XLA Ops:
  0.0 3.5 %synth.1 = bf16[256,128]{1,0:T(8,128)(2,1)} custom-call(bf16[2,48,2048]{2,1,0:T(8,128)(2,1)} %bitcast.8, bf16[2,2,256,2048]{3,2,1,0:T(8,128)(2,1)} %tab_hbm.3, f32[1,2048]{1,0:T(1,128)} %beam_ref.1), custom_call_target="tpu_custom_call" | custom-call | tf_op jit(solution)/shard_map/synth/pallas_call | solution.py:83
  3.5 0.0 copy-start.1
  3.5 0.0 copy-start.2
  3.5 0.0 copy-start.3
  3.5 0.0 copy-start.7
  3.6 13.8 %all-to-all-start = ((bf16[32,8,128]{2,1,0:T(8,128)(2,1)}), bf16[32,8,128]{2,1,0:T(8,128)(2,1)S(1)}, u32[]{:S(2)}, u32[]{:S(2)}) async-start(bf16[32,8,128]{2,1,0:T(8,128)(2,1)} %bitcast.3), calls=%async_computation | async-start | bytes 131072 | tf_op jit(solution)/shard_map/all_to_all | solution.py:384
  17.4 0.0 copy-done.6
  17.4 2.5 %phase_table.1.tab_ref = bf16[256,4096]{1,0:T(8,128)(2,1)S(1)} custom-call(s32[64]{0:T(128)S(1)} %copy-done.6), custom_call_target="tpu_custom_call" | custom-call | flops 8000000 | bytes 2097152 | tf_op jit(solution)/shard_map/phase_table/pallas_call | solution.py:151
  20.0 0.0 copy-start.4
  20.0 6.3 %all-to-all-done = bf16[32,8,128]{2,1,0:T(8,128)(2,1)S(1)} async-done(((bf16[32,8,128]{2,1,0:T(8,128)(2,1)}), bf16[32,8,128]{2,1,0:T(8,128)(2,1)S(1)}, u32[]{:S(2)}, u32[]{:S(2)}) %all-to-all-start) | async-done | bytes 65568 | tf_op jit(solution)/shard_map/all_to_all | solution.py:384
  26.2 0.0 copy-done.1
  26.3 2.9 %pixels.1 = bf16[2,256,128]{2,1,0:T(8,128)(2,1)} custom-call(s32[8]{0:T(128)S(1)} %copy-done.7, bf16[256,128]{1,0:T(8,128)(2,1)S(1)} %bitcast.11, bf16[256,4096]{1,0:T(8,128)(2,1)S(1)} %phase_table.1.tab_ref, f32[1,3,8,4096]{3,2,1,0:T(8,128)S(1)} %copy-done.1, f32[1,2,8,4096]{3,2,1,0:T(8,128)S(1)} %copy-done.2, f32[1,8,4096]{2,1,0:T(8,128)S(1)} %copy-done.3), custom_call_target="tpu_custom_call" | custom-call | tf_op jit(solution)/shard_map/pixels/pallas_call | solution.py:252
  29.1 6.3 %all-to-all-start.1 = ((bf16[64,8,128]{2,1,0:T(8,128)(2,1)}), bf16[64,8,128]{2,1,0:T(8,128)(2,1)S(1)}, u32[]{:S(2)}, u32[]{:S(2)}) async-start(bf16[64,8,128]{2,1,0:T(8,128)(2,1)} %bitcast.5), calls=%async_computation.1 | async-start | bytes 262144 | tf_op jit(solution)/shard_map/all_to_all | solution.py:387
  35.5 0.0 copy-done.4
  35.5 1.6 %fetch.1 = (bf16[2,2,256,1024]{3,2,1,0:T(8,128)(2,1)S(1)}, f32[1,1024]{1,0:T(1,128)S(1)}, f32[1,1024]{1,0:T(1,128)S(1)}) custom-call(s32[1]{0:T(128)} %bitcast.1.core_ref, bf16[2,2,256,2048]{3,2,1,0:T(8,128)(2,1)} %tab_hbm.3, f32[1,2048]{1,0:T(1,128)S(1)} %copy-done.4), custom_call_target="tpu_custom_call" | custom-call | bytes 4194304 | tf_op jit(solution)/shard_map/fetch/pallas_call | solution.py:287
  37.2 0.0 copy-start
  37.2 0.0 copy-start.5
  37.2 2.4 %collective-permute-start = (f32[1,1024]{1,0:T(1,128)S(1)}, f32[1,1024]{1,0:T(1,128)S(1)}, u32[]{:S(2)}, u32[]{:S(2)}) collective-permute-start(f32[1,1024]{1,0:T(1,128)S(1)} %get-tuple-element.10), channel_id=1, source_target_pairs={{0,32},{32,0},{1,33},{33,1},{2,34},{34,2},{3,35},{35,3},{4,36},{36... | collective-permute-start | bytes 12296 | tf_op jit(solution)/shard_map/ppermute | solution.py:391
  39.6 0.8 %collective-permute-done.other_ref = f32[1,1024]{1,0:T(1,128)S(1)} collective-permute-done((f32[1,1024]{1,0:T(1,128)S(1)}, f32[1,1024]{1,0:T(1,128)S(1)}, u32[]{:S(2)}, u32[]{:S(2)}) %collective-permute-start) | collective-permute-done | bytes 4128 | tf_op jit(solution)/shard_map/ppermute | solution.py:391
  40.4 5.6 %all-to-all-done.1 = bf16[64,8,128]{2,1,0:T(8,128)(2,1)S(1)} async-done(((bf16[64,8,128]{2,1,0:T(8,128)(2,1)}), bf16[64,8,128]{2,1,0:T(8,128)(2,1)S(1)}, u32[]{:S(2)}, u32[]{:S(2)}) %all-to-all-start.1) | async-done | bytes 131104 | tf_op jit(solution)/shard_map/all_to_all | solution.py:387
  46.0 1.2 %adjoint.1 = bf16[8,2,48,128]{3,2,1,0:T(8,128)(2,1)} custom-call(s32[1]{0:T(128)} %bitcast.1.core_ref, bf16[2,256,128]{2,1,0:T(8,128)(2,1)S(1)} %bitcast.10, bf16[2,2,256,1024]{3,2,1,0:T(8,128)(2,1)S(1)} %get-tuple-element.8.tab_ref, f32[1,1024]{1,0:T(1,128)S(1)} %get-tuple-element.9.own_ref, f32[1,1024]{1,0:T(1,128)S(1)} %collective-permute-done.other_ref), custom_call_target="tpu_custom_call" | custom-call | tf_op jit(solution)/shard_map/adjoint/pallas_call | solution.py:334
  47.2 6.8 %all-to-all-start.2 = ((bf16[8,2,48,128]{3,2,1,0:T(8,128)(2,1)}), bf16[8,2,48,128]{3,2,1,0:T(8,128)(2,1)S(1)}, u32[]{:S(2)}, u32[]{:S(2)}) async-start(bf16[8,2,48,128]{3,2,1,0:T(8,128)(2,1)} %adjoint.1), calls=%async_computation.2 | async-start | bytes 393216 | tf_op jit(solution)/shard_map/all_to_all | solution.py:393
  54.0 10.9 %all-to-all-done.2.sum_ref = bf16[8,2,48,128]{3,2,1,0:T(8,128)(2,1)S(1)} async-done(((bf16[8,2,48,128]{3,2,1,0:T(8,128)(2,1)}), bf16[8,2,48,128]{3,2,1,0:T(8,128)(2,1)S(1)}, u32[]{:S(2)}, u32[]{:S(2)}) %all-to-all-start.2) | async-done | bytes 196640 | tf_op jit(solution)/shard_map/all_to_all | solution.py:393
  65.0 0.7 %final.1 = f32[2,48,128]{2,1,0:T(8,128)} custom-call(s32[1]{0:T(128)} %bitcast.band_ref, bf16[8,2,48,128]{3,2,1,0:T(8,128)(2,1)S(1)} %all-to-all-done.2.sum_ref, bf16[2,48,2048]{2,1,0:T(8,128)(2,1)S(1)} %bitcast.9, f32[6,128]{1,0:T(8,128)S(1)} %copy-done.5), custom_call_target="tpu_custom_call" | custom-call | tf_op jit(solution)/shard_map/final/pallas_call | solution.py:363
  (6 shorter events, 0.0 us)
Async XLA Ops:
  0.0 17.4 %copy-start.6 = (s32[64]{0:T(128)S(1)}, s32[64]{0:T(128)}, u32[]{:S(2)}) copy-start(s32[64]{0:T(128)} %m_ref.1) | copy-start | bytes 772
  3.5 22.7 %copy-start.1 = (f32[1,3,8,4096]{3,2,1,0:T(8,128)S(1)}, f32[1,3,8,4096]{3,2,1,0:T(8,128)}, u32[]{:S(2)}) copy-start(f32[1,3,8,4096]{3,2,1,0:T(8,128)} %mix_ref.1) | copy-start | bytes 1179652
  3.5 22.7 %copy-start.2 = (f32[1,2,8,4096]{3,2,1,0:T(8,128)S(1)}, f32[1,2,8,4096]{3,2,1,0:T(8,128)}, u32[]{:S(2)}) copy-start(f32[1,2,8,4096]{3,2,1,0:T(8,128)} %diag_ref.1) | copy-start | bytes 786436
  3.5 22.7 %copy-start.3 = (f32[1,8,4096]{2,1,0:T(8,128)S(1)}, f32[1,8,4096]{2,1,0:T(8,128)}, u32[]{:S(2)}) copy-start(f32[1,8,4096]{2,1,0:T(8,128)} %cross_ref.1) | copy-start | bytes 393220
  3.5 22.7 %copy-start.7 = (s32[8]{0:T(128)S(1)}, s32[8]{0:T(128)}, u32[]{:S(2)}) copy-start(s32[8]{0:T(128)} %ids_ref.1) | copy-start | bytes 100
  3.6 22.7 %all-to-all-start = ((bf16[32,8,128]{2,1,0:T(8,128)(2,1)}), bf16[32,8,128]{2,1,0:T(8,128)(2,1)S(1)}, u32[]{:S(2)}, u32[]{:S(2)}) async-start(bf16[32,8,128]{2,1,0:T(8,128)(2,1)} %bitcast.3), calls=%async_computation | async-start | bytes 131072 | tf_op jit(solution)/shard_map/all_to_all | solution.py:384
  20.0 15.6 %copy-start.4 = (f32[1,2048]{1,0:T(1,128)S(1)}, f32[1,2048]{1,0:T(1,128)}, u32[]{:S(2)}) copy-start(f32[1,2048]{1,0:T(1,128)} %beam_ref.1) | copy-start | bytes 24580
  29.1 16.8 %all-to-all-start.1 = ((bf16[64,8,128]{2,1,0:T(8,128)(2,1)}), bf16[64,8,128]{2,1,0:T(8,128)(2,1)S(1)}, u32[]{:S(2)}, u32[]{:S(2)}) async-start(bf16[64,8,128]{2,1,0:T(8,128)(2,1)} %bitcast.5), calls=%async_computation.1 | async-start | bytes 262144 | tf_op jit(solution)/shard_map/all_to_all | solution.py:387
  37.2 27.8 %copy-start = (bf16[2,2048,48]{1,2,0:T(8,128)(2,1)S(1)}, bf16[2,2048,48]{1,2,0:T(8,128)(2,1)}, u32[]{:S(2)}) copy-start(bf16[2,2048,48]{1,2,0:T(8,128)(2,1)} %param.9) | copy-start | bytes 1179652
  37.2 27.8 %copy-start.5 = (f32[6,128]{1,0:T(8,128)S(1)}, f32[6,128]{1,0:T(8,128)}, u32[]{:S(2)}) copy-start(f32[6,128]{1,0:T(8,128)} %prior_ref.1) | copy-start | bytes 9220
  37.2 3.2 %collective-permute-start = (f32[1,1024]{1,0:T(1,128)S(1)}, f32[1,1024]{1,0:T(1,128)S(1)}, u32[]{:S(2)}, u32[]{:S(2)}) collective-permute-start(f32[1,1024]{1,0:T(1,128)S(1)} %get-tuple-element.10), channel_id=1, source_target_pairs={{0,32},{32,0},{1,33},{33,1},{2,34},{34,2},{3,35},{35,3},{4,36},{36... | collective-permute-start | bytes 12296 | tf_op jit(solution)/shard_map/ppermute | solution.py:391
  47.2 17.8 %all-to-all-start.2 = ((bf16[8,2,48,128]{3,2,1,0:T(8,128)(2,1)}), bf16[8,2,48,128]{3,2,1,0:T(8,128)(2,1)S(1)}, u32[]{:S(2)}, u32[]{:S(2)}) async-start(bf16[8,2,48,128]{3,2,1,0:T(8,128)(2,1)} %adjoint.1), calls=%async_computation.2 | async-start | bytes 393216 | tf_op jit(solution)/shard_map/all_to_all | solution.py:393

commit v3 on v2

v3 whole, which is shorter than its diff:
```python
import math

import jax
import jax.numpy as jnp
from jax import lax
from jax.experimental import pallas as pl
from jax.experimental.pallas import tpu as pltpu
from jax.sharding import Mesh
from jax.sharding import PartitionSpec as P

F32 = jnp.float32
BF16 = jnp.bfloat16

PIX = 4096
COMPS = 3
CHAINS = 4
PAIRS = CHAINS * COMPS
COLS = 4 * PAIRS
WIDE = 64
PER = 8

NT = (((1,), (1,)), ((), ()))
NN = (((1,), (0,)), ((), ()))


def grant(mib):
    return pltpu.CompilerParams(vmem_limit_bytes=mib << 20)


def iota(shape, dim):
    return lax.broadcasted_iota(jnp.int32, shape, dim)


def dot(a, b, dims):
    return lax.dot_general(a, b, dims, preferred_element_type=F32)


SIGN = (-1.0, 1.0, 1.0, -1.0)


CHUNKS = 4


def synth_kernel(
    coef_hbm, tab_hbm, beam_hbm, out_ref, coef_ref, tab_ref, beam_ref, rows_ref, nat_ref, cross_ref, sems
):
    levels = coef_ref.shape[2]
    width = levels // CHUNKS
    head = pltpu.make_async_copy(beam_hbm, beam_ref, sems.at[2, 0])
    head.start()
    copies = []
    for c in range(CHUNKS):
        at = pl.ds(c * width, width)
        copies.append(
            (
                pltpu.make_async_copy(coef_hbm.at[:, :, at], coef_ref.at[:, :, at], sems.at[0, c]),
                pltpu.make_async_copy(tab_hbm.at[:, :, :, at], tab_ref.at[c], sems.at[1, c]),
            )
        )
        for copy in copies[c]:
            copy.start()
    rows_ref[:, :, COLS:, :] = jnp.zeros_like(rows_ref[:, :, COLS:, :])
    head.wait()

    def prepare(c):
        copies[c][0].wait()
        for s in range(2):
            for j in range(c * width // 128, (c + 1) * width // 128):
                at = slice(j * 128, (j + 1) * 128)
                beamed = (coef_ref[s, :, at].astype(F32) * beam_ref[:, at]).astype(BF16)
                rows_ref[s, 0, :COLS, at] = beamed
                nat_ref[s, j] = beamed.astype(F32)
                for k in range(4):
                    value = nat_ref[s, j, pl.ds(3 - k, PAIRS, stride=4), :]
                    cross_ref[s, j, pl.ds(k, PAIRS, stride=4), :] = SIGN[k] * value
                rows_ref[s, 1, :COLS, at] = cross_ref[s, j].astype(BF16)

    prepare(0)
    total = [None, None]
    for c in range(CHUNKS):
        copies[c][1].wait()
        if c + 1 < CHUNKS:
            prepare(c + 1)
        for s in range(2):
            for which in range(2):
                rows = rows_ref[s, which, :, c * width : (c + 1) * width]
                part = dot(tab_ref[c, s, which], rows, NT)
                total[s] = part if total[s] is None else total[s] + part
    out_ref[...] = jnp.concatenate(total, 1).astype(BF16)


def synth(coeffs_t, tables, beam):
    _, cols, levels = coeffs_t.shape
    cycles = tables.shape[2]
    hbm = pl.BlockSpec(memory_space=pltpu.HBM)
    vmem = pl.BlockSpec(memory_space=pltpu.VMEM)
    return pl.pallas_call(
        synth_kernel,
        out_shape=jax.ShapeDtypeStruct((cycles, 128), BF16),
        in_specs=[hbm] * 3,
        out_specs=vmem,
        scratch_shapes=[
            pltpu.VMEM((2, cols, levels), BF16),
            pltpu.VMEM((CHUNKS, 2, 2, cycles, levels // CHUNKS), BF16),
            pltpu.VMEM((1, levels), F32),
            pltpu.VMEM((2, 2, WIDE, levels), BF16),
            pltpu.VMEM((2, levels // 128, COLS, 128), F32),
            pltpu.VMEM((2, levels // 128, COLS, 128), F32),
            pltpu.SemaphoreType.DMA((3, CHUNKS)),
        ],
        compiler_params=grant(12),
        name="synth",
    )(coeffs_t, tables, beam)


def table_kernel(m_ref, out_ref, perm_ref):
    row, col = iota(perm_ref.shape, 0), iota(perm_ref.shape, 1)
    field = row // PER
    upper = (field >= PAIRS).astype(jnp.int32)
    target = (row % PER) * (WIDE // 2) + 2 * (field - PAIRS * upper) + upper
    perm_ref[...] = jnp.where((col >> 1) == target, 1.0, 0.0).astype(BF16)

    quarter = PIX // 4
    row = iota((32, 128), 0)
    mode, gain = [], []
    for s in range(2):
        m = jnp.zeros((32, 128), jnp.int32)
        for j in range(32):
            m = jnp.where(row == j, m_ref[2 * j + s], m)
        mode.append(m)
        gain.append(jnp.where(m == 0, 1.0, 2.0).astype(F32))
    lane = iota((32, 128), 1)

    def chunk(i, carry):
        first = i * 128
        for par in range(2):
            for s in range(2):
                k = (mode[s] * (2 * (lane + first) + par)) & (2 * PIX - 1)
                n = (k + quarter) >> 11
                angle = (k - (n << 11)).astype(F32) * F32(math.pi / PIX)
                sq = angle * angle
                c = -1 / 3628800
                for inv in (1 / 40320, -1 / 720, 1 / 24, -1 / 2, 1.0):
                    c = c * sq + F32(inv)
                d = 1 / 362880
                for inv in (-1 / 5040, 1 / 120, -1 / 6, 1.0):
                    d = d * sq + F32(inv)
                d = d * angle
                swap = (n & 1) == 1
                cosine = jnp.where(swap, d, c)
                sine = jnp.where(swap, c, d)
                cosine = jnp.where(((n + 1) & 2) == 2, -cosine, cosine)
                sine = jnp.where((n & 2) == 2, -sine, sine)
                for reim in range(2):
                    top = par * 128 + (2 * reim + s) * 32
                    for u in range(4):
                        turn = (mode[s] * u + reim) & 3
                        value = jnp.where((turn & 1) == 1, sine, cosine)
                        scale = jnp.where(((turn + 1) & 2) == 2, -gain[s], gain[s])
                        at = pl.ds(pl.multiple_of(u * quarter + first, 128), 128)
                        out_ref[top : top + 32, at] = (value * scale).astype(BF16)
        return carry

    lax.fori_loop(0, quarter // 128, chunk, 0)


def phase_table(m_values):
    return pl.pallas_call(
        table_kernel,
        out_shape=(
            jax.ShapeDtypeStruct((256, PIX), BF16),
            jax.ShapeDtypeStruct((2 * PAIRS * PER, WIDE * PER), BF16),
        ),
        in_specs=[pl.BlockSpec(memory_space=pltpu.SMEM)],
        out_specs=[pl.BlockSpec(memory_space=pltpu.VMEM)] * 2,
        cost_estimate=pl.CostEstimate(flops=8_000_000, bytes_accessed=2_097_152, transcendentals=0),
        compiler_params=grant(6),
        name="phase_table",
    )(m_values)


def by_cycle(values, place):
    odd = jnp.zeros(place.shape, jnp.int32)
    for t in range(PER):
        odd = jnp.where(place == t, values[t], odd)
    return odd == 1


def pixel_kernel(
    ids_ref, x_ref, tab_ref, perm_ref, mix_ref, diag_ref, cross_ref, out_ref, rows_ref, acc_ref
):
    parity = [ids_ref[t] & 1 for t in range(PER)]
    lane = iota((32, 128), 1)
    left = lane < WIDE
    rows_ref[...] = x_ref[...].astype(F32)
    tiles = []
    for u in range(PER // 2):
        pair = [rows_ref[pl.ds(2 * u + i, 32, stride=PER), :] for i in range(2)]
        swapped = [pltpu.roll(v, WIDE, 1) for v in pair]
        modes = [jnp.where(left, pair[0], swapped[1]), jnp.where(left, swapped[0], pair[1])]
        tiles.append(
            jnp.concatenate(
                [jnp.where((lane & 1) == reim, v, 0.0) for reim in range(2) for v in modes], 0
            )
        )
    gathered = jnp.concatenate(tiles, 1).astype(BF16)

    lhs = dot(perm_ref[...], gathered, NT)
    odd_row = by_cycle(parity, iota(lhs.shape, 0) % PER)
    zero = jnp.zeros_like(lhs)
    lhs = jnp.concatenate(
        [jnp.where(odd_row, zero, lhs), jnp.where(odd_row, lhs, zero)], 1
    ).astype(BF16)

    width = 2048
    for p in range(PIX // width):
        at = slice(p * width, (p + 1) * width)
        table = tab_ref[:, at]
        maps = dot(lhs, table, NN)
        mix = [mix_ref[0, c, :, at] for c in range(COMPS)]
        diag = [diag_ref[0, e, :, at] for e in range(2)]
        cross = cross_ref[0, :, at]
        back = [[None] * PAIRS, [None] * PAIRS]
        for chain in range(CHAINS):
            sky = []
            for e in range(2):
                total = None
                for c in range(COMPS):
                    f = e * PAIRS + chain * COMPS + c
                    part = maps[f * PER : (f + 1) * PER] * mix[c]
                    total = part if total is None else total + part
                sky.append(total)
            weighted = [
                diag[0] * sky[0] + cross * sky[1],
                cross * sky[0] + diag[1] * sky[1],
            ]
            for e in range(2):
                for c in range(COMPS):
                    back[e][chain * COMPS + c] = weighted[e] * mix[c]
        back = jnp.concatenate(back[0] + back[1], 0).astype(BF16)
        part = dot(table, back, NT)
        if p == 0:
            acc_ref[...] = part
        else:
            acc_ref[...] += part

    odd_lane = by_cycle(parity, iota((128, acc_ref.shape[1]), 1) % PER)
    returned = jnp.where(odd_lane, acc_ref[128:, :], acc_ref[:128, :]).astype(BF16)
    spread = dot(returned, perm_ref[...], NN)
    for u in range(PER // 2):
        tile = spread[:, u * 128 : (u + 1) * 128]
        modes = [
            jnp.where((lane & 1) == 1, tile[64 + s * 32 : 96 + s * 32], tile[s * 32 : 32 + s * 32])
            for s in range(2)
        ]
        swapped = [pltpu.roll(v, WIDE, 1) for v in modes]
        rows_ref[pl.ds(2 * u, 32, stride=PER), :] = jnp.where(left, modes[0], swapped[1])
        rows_ref[pl.ds(2 * u + 1, 32, stride=PER), :] = jnp.where(left, swapped[0], modes[1])
    result = rows_ref[...].astype(BF16)
    out_ref[0] = result
    out_ref[1] = result


def pixels(cycle_ids, arrived, table, perm, mixing, noise_diag, noise_cross):
    vmem = pl.BlockSpec(memory_space=pltpu.VMEM)
    return pl.pallas_call(
        pixel_kernel,
        out_shape=jax.ShapeDtypeStruct((2, 256, 128), BF16),
        in_specs=[pl.BlockSpec(memory_space=pltpu.SMEM)] + [vmem] * 6,
        out_specs=vmem,
        scratch_shapes=[pltpu.VMEM((256, 128), F32), pltpu.VMEM((256, 2 * PAIRS * PER), F32)],
        compiler_params=grant(10),
        name="pixels",
    )(cycle_ids, arrived, table, perm, mixing, noise_diag, noise_cross)


def fetch_kernel(place_ref, tab_hbm, beam_ref, out_ref, own_ref, sent_ref, sems):
    blocks = tab_hbm.shape[3] // 256
    copies = []
    for k in range(blocks):
        source = pl.ds(pl.multiple_of(256 * k + 128 * place_ref[0], 128), 128)
        place = pl.ds(128 * k, 128)
        copies.append(
            pltpu.make_async_copy(
                tab_hbm.at[:, :, :, source], out_ref.at[:, :, :, place], sems.at[k]
            )
        )
        copies[-1].start()
        pair = [beam_ref[:, (2 * k + c) * 128 : (2 * k + c + 1) * 128] for c in range(2)]
        second = place_ref[0] == 1
        own_ref[:, 128 * k : 128 * (k + 1)] = jnp.where(second, pair[1], pair[0])
        sent_ref[:, 128 * k : 128 * (k + 1)] = jnp.where(second, pair[0], pair[1])
    for copy in copies:
        copy.wait()


def fetch(place, tables, beam):
    levels = tables.shape[3]
    hbm = pl.BlockSpec(memory_space=pltpu.HBM)
    vmem = pl.BlockSpec(memory_space=pltpu.VMEM)
    return pl.pallas_call(
        fetch_kernel,
        out_shape=(
            jax.ShapeDtypeStruct(tables.shape[:3] + (levels // 2,), BF16),
            jax.ShapeDtypeStruct((1, levels // 2), F32),
            jax.ShapeDtypeStruct((1, levels // 2), F32),
        ),
        in_specs=[pl.BlockSpec(memory_space=pltpu.SMEM), hbm, vmem],
        out_specs=(vmem, vmem, vmem),
        scratch_shapes=[pltpu.SemaphoreType.DMA((levels // 256,))],
        compiler_params=grant(4),
        cost_estimate=pl.CostEstimate(flops=0, bytes_accessed=4_194_304, transcendentals=0),
        name="fetch",
    )(place, tables, beam)


def adjoint_kernel(
    place_ref, r_ref, tab_ref, own_ref, other_ref, out_ref, lhs_ref, plain_ref, cross_ref
):
    for b, index in enumerate((place_ref[0], 1 - place_ref[0])):
        for h in range(2):
            half = slice(h * 128, (h + 1) * 128)
            plain_ref[b, h] = r_ref[index, half, :].astype(F32).T
            for k in range(4):
                value = plain_ref[b, h, pl.ds(3 - k, 32, stride=4), :]
                cross_ref[b, h, pl.ds(k, 32, stride=4), :] = SIGN[k] * value
            for s in range(2):
                at = slice(b * COLS, (b + 1) * COLS)
                rows = slice(s * WIDE, s * WIDE + COLS)
                lhs_ref[s, 0, at, half] = plain_ref[b, h, rows, :].astype(BF16)
                lhs_ref[s, 1, at, half] = cross_ref[b, h, rows, :].astype(BF16)

    width = 256
    for s in range(2):
        for k in range(tab_ref.shape[3] // width):
            at = slice(k * width, (k + 1) * width)
            sums = dot(lhs_ref[s, 0], tab_ref[s, 0, :, at], NN) + dot(
                lhs_ref[s, 1], tab_ref[s, 1, :, at], NN
            )
            sums = (sums[:COLS] * own_ref[:, at] + sums[COLS:] * other_ref[:, at]).astype(BF16)
            for h in range(width // 128):
                out_ref[k * (width // 128) + h, s] = sums[:, h * 128 : (h + 1) * 128]


def adjoint(place, returned, tables, own_beam, other_beam):
    cycles, levels = tables.shape[2:]
    blocks = levels // 128
    vmem = pl.BlockSpec(memory_space=pltpu.VMEM)
    return pl.pallas_call(
        adjoint_kernel,
        out_shape=jax.ShapeDtypeStruct((blocks, 2, COLS, 128), BF16),
        in_specs=[pl.BlockSpec(memory_space=pltpu.SMEM)] + [vmem] * 4,
        out_specs=vmem,
        scratch_shapes=[
            pltpu.VMEM((2, 2, 2 * COLS, cycles), BF16),
            pltpu.VMEM((2, 2, 128, 128), F32),
            pltpu.VMEM((2, 2, 128, 128), F32),
        ],
        compiler_params=grant(8),
        name="adjoint",
    )(place, returned, tables, own_beam, other_beam)


def final_kernel(place_ref, sum_ref, coef_ref, prior_ref, out_ref):
    kind = iota((COLS, 128), 0) % (4 * COMPS) // 2
    prior = jnp.zeros((COLS, 128), F32)
    for k in range(2 * COMPS):
        prior = jnp.where(kind == k, prior_ref[k : k + 1, :], prior)
    at = pl.ds(pl.multiple_of(128 * place_ref[1], 128), 128)
    for s in range(2):
        total = prior * coef_ref[s, :, at].astype(F32)
        for y in range(sum_ref.shape[0]):
            total = total + sum_ref[y, s].astype(F32)
        out_ref[s] = total


def final(place, gathered, coeffs_t, prior):
    vmem = pl.BlockSpec(memory_space=pltpu.VMEM)
    return pl.pallas_call(
        final_kernel,
        out_shape=jax.ShapeDtypeStruct((2, COLS, 128), F32),
        in_specs=[pl.BlockSpec(memory_space=pltpu.SMEM)] + [vmem] * 3,
        out_specs=vmem,
        compiler_params=grant(4),
        name="final",
    )(place, gathered, coeffs_t, prior)


def on_device(coeffs, tables, beam, mixing, noise_diag, noise_cross, prior, m_values, cycle_ids):
    core = lax.axis_index("core")
    place = jnp.stack([core, 2 * lax.axis_index("y") + core]).astype(jnp.int32)
    coeffs_t = coeffs.transpose(0, 2, 1)
    stored = pltpu.with_memory_space_constraint(tables, pltpu.HBM)
    spectra = synth(
        pltpu.with_memory_space_constraint(coeffs_t, pltpu.HBM),
        stored,
        pltpu.with_memory_space_constraint(beam, pltpu.HBM),
    )
    arrived = lax.all_to_all(spectra.reshape(32, PER, 128), "ma", 0, 0, tiled=True)
    table, perm = phase_table(m_values)
    returned = pixels(cycle_ids, arrived.reshape(256, 128), table, perm, mixing, noise_diag, noise_cross)
    returned = lax.all_to_all(
        returned.reshape(64, PER, 128), ("core", "ma"), 0, 0, tiled=True
    ).reshape(2, 256, 128)
    level_tables, own_beam, sent_beam = fetch(place, stored, beam)
    other_beam = lax.ppermute(sent_beam, "core", [(0, 1), (1, 0)])
    partial = adjoint(place, returned, level_tables, own_beam, other_beam)
    gathered = lax.all_to_all(partial, "y", 0, 0, tiled=True)
    return final(place, gathered, coeffs_t, prior).transpose(0, 2, 1)


def solution(mesh):
    bands, modes = mesh.devices.shape
    fine = Mesh(mesh.devices.reshape(bands // 2, 2, modes), ("y", "core", "ma"))
    band = ("y", "core")
    in_specs = (
        P("ma", None, None),
        P("ma", None, None, None),
        P(band, None),
        P(band, None, "ma", None),
        P(band, None, "ma", None),
        P(band, "ma", None),
        P(None, band),
        P(),
        P("ma"),
    )
    return jax.shard_map(
        on_device, mesh=fine, in_specs=in_specs, out_specs=P("ma", band, None), check_vma=False
    )
```

time: 66 us -> 66.3 us (level)
  blocking collectives: 0 us -> 17.6 us
  waiting for transfers between devices: 23.6 us -> 12 us
  starting transfers between devices: 29.4 us -> 22.5 us
  Pallas kernels: 12.5 us -> 13.7 us
    all_to_all x0 -> x1, blocking collectives: none -> 17.6 us  [on_device(): gathered = lax.all_to_all(partial, 'y', 0, 0, tiled=True)]
    all_to_all x1 -> x0, waiting for transfers between devices: 10.9 us -> none  [on_device(): gathered = lax.all_to_all(partial, 'y', 0, 0, tiled=True)]
    all_to_all x1 -> x0, starting transfers between devices: 6.82 us -> none  [on_device(): gathered = lax.all_to_all(partial, 'y', 0, 0, tiled=True)]
  transfers between devices with their start and end apart: 4 -> 3, of which waited for: 4 -> 3; matrix products, arithmetic and copies ran while one was open for 0% -> 0% of each run, Pallas kernels for 6% -> 7%
where the time goes in v3:
time: 66.3 us; the launch traced here: 66 us
  starting transfers between devices  22.5 us (34%)
  blocking collectives  17.6 us (27%)
  Pallas kernels  13.7 us (21%)
  waiting for transfers between devices  12 us (18%)
    all_to_all x1, blocking collectives, on_device(): gathered = lax.all_to_all(partial, 'y', 0, 0, tiled=True)  17.6 us
    all_to_all x1, starting transfers between devices, on_device(): lax.all_to_all(spectra.reshape(32, PER, 128), 'ma', 0, 0, tiled=True)  13.7 us
    all_to_all x1, starting transfers between devices, on_device(): lax.all_to_all(returned.reshape(64, PER, 128), ('core', 'ma'), 0, 0, tile...  6.35 us
    all_to_all x1, waiting for transfers between devices, on_device(): lax.all_to_all(spectra.reshape(32, PER, 128), 'ma', 0, 0, tiled=True)  6.23 us
    all_to_all x1, waiting for transfers between devices, on_device(): lax.all_to_all(returned.reshape(64, PER, 128), ('core', 'ma'), 0, 0, tile...  4.97 us
    pallas_call x1, Pallas kernels, synth(): pl.pallas_call(synth_kernel, out_shape=jax.ShapeDtypeStruct((cycles, 128)...  3.7 us
    pallas_call x1, Pallas kernels, pixels(): pl.pallas_call(pixel_kernel, out_shape=jax.ShapeDtypeStruct((2, 256, 128)...  2.94 us
    pallas_call x1, Pallas kernels, phase_table(): pl.pallas_call(table_kernel, out_shape=(jax.ShapeDtypeStruct((256, PIX),...  2.57 us
  transfers between devices with their start and end apart: 3, of which 3 were waited for; matrix products, arithmetic and copies ran while one was open for 0% of the time, Pallas kernels for 7%

profile of v3, /device:TPU:1, one launch (start us, length us, event | category | flops | bytes accessed | tf_op | source)
XLA Modules:
  0.0 66.0 jit_solution(12469931037915382778)
XLA Ops:
  0.0 0.0 copy-start.3
  0.0 0.0 copy-start.6
  0.0 3.7 %synth.1 = bf16[256,128]{1,0:T(8,128)(2,1)} custom-call(bf16[2,48,2048]{2,1,0:T(8,128)(2,1)} %bitcast.8, bf16[2,2,256,2048]{3,2,1,0:T(8,128)(2,1)} %tab_hbm.3, f32[1,2048]{1,0:T(1,128)} %beam_ref.1), custom_call_target="tpu_custom_call" | custom-call | tf_op jit(solution)/shard_map/synth/pallas_call | solution.py:97
  3.7 0.0 copy-start.4
  3.7 13.7 %all-to-all-start = ((bf16[32,8,128]{2,1,0:T(8,128)(2,1)}), bf16[32,8,128]{2,1,0:T(8,128)(2,1)S(1)}, u32[]{:S(2)}, u32[]{:S(2)}) async-start(bf16[32,8,128]{2,1,0:T(8,128)(2,1)} %bitcast.3), calls=%async_computation | async-start | bytes 131072 | tf_op jit(solution)/shard_map/all_to_all | solution.py:399
  17.5 0.0 copy-done.7
  17.5 2.6 %phase_table.1 = (bf16[256,4096]{1,0:T(8,128)(2,1)S(1)}, bf16[192,512]{1,0:T(8,128)(2,1)S(1)}) custom-call(s32[64]{0:T(128)S(1)} %copy-done.7), custom_call_target="tpu_custom_call" | custom-call | flops 8000000 | bytes 2097152 | tf_op jit(solution)/shard_map/phase_table/pallas_call | solution.py:168
  20.1 6.2 %all-to-all-done = bf16[32,8,128]{2,1,0:T(8,128)(2,1)S(1)} async-done(((bf16[32,8,128]{2,1,0:T(8,128)(2,1)}), bf16[32,8,128]{2,1,0:T(8,128)(2,1)S(1)}, u32[]{:S(2)}, u32[]{:S(2)}) %all-to-all-start) | async-done | bytes 65568 | tf_op jit(solution)/shard_map/all_to_all | solution.py:399
  26.3 0.0 copy-done.1
  26.3 0.0 copy-done.2
  26.3 0.0 copy-done.3
  26.3 2.9 %pixels.1 = bf16[2,256,128]{2,1,0:T(8,128)(2,1)} custom-call(s32[8]{0:T(128)S(1)} %copy-done.6, bf16[256,128]{1,0:T(8,128)(2,1)S(1)} %bitcast.11, bf16[256,4096]{1,0:T(8,128)(2,1)S(1)} %get-tuple-element.10.tab_ref, bf16[192,512]{1,0:T(8,128)(2,1)S(1)} %get-tuple-element.11.perm_ref, f32[1,3,8,4096]{3,2,1,0:T(8,128)S(1)} %copy-done.1, ...), custom_call_target="tpu_custom_call" | custom-call | tf_op jit(solution)/shard_map/pixels/pallas_call | solution.py:266
  29.3 6.4 %all-to-all-start.1 = ((bf16[64,8,128]{2,1,0:T(8,128)(2,1)}), bf16[64,8,128]{2,1,0:T(8,128)(2,1)S(1)}, u32[]{:S(2)}, u32[]{:S(2)}) async-start(bf16[64,8,128]{2,1,0:T(8,128)(2,1)} %bitcast.5), calls=%async_computation.1 | async-start | bytes 262144 | tf_op jit(solution)/shard_map/all_to_all | solution.py:402
  35.6 0.1 pad_add_fusion.place_ref
  35.7 0.0 copy-done.4
  35.7 2.2 %fetch.1 = (bf16[2,2,256,1024]{3,2,1,0:T(8,128)(2,1)S(1)}, f32[1,1024]{1,0:T(1,128)S(1)}, f32[1,1024]{1,0:T(1,128)S(1)}) custom-call(s32[2]{0:T(128)S(1)} %pad_add_fusion.place_ref, bf16[2,2,256,2048]{3,2,1,0:T(8,128)(2,1)} %tab_hbm.3, f32[1,2048]{1,0:T(1,128)S(1)} %copy-done.4), custom_call_target="tpu_custom_call" | custom-call | bytes 4194304 | tf_op jit(solution)/shard_map/fetch/pallas_call | solution.py:301
  37.9 0.0 copy-start
  37.9 0.0 copy-start.5
  37.9 2.4 %collective-permute-start = (f32[1,1024]{1,0:T(1,128)S(1)}, f32[1,1024]{1,0:T(1,128)S(1)}, u32[]{:S(2)}, u32[]{:S(2)}) collective-permute-start(f32[1,1024]{1,0:T(1,128)S(1)} %get-tuple-element.14), channel_id=1, source_target_pairs={{0,32},{32,0},{1,33},{33,1},{2,34},{34,2},{3,35},{35,3},{4,36},{36... | collective-permute-start | bytes 12296 | tf_op jit(solution)/shard_map/ppermute | solution.py:406
  40.3 0.8 %collective-permute-done.other_ref = f32[1,1024]{1,0:T(1,128)S(1)} collective-permute-done((f32[1,1024]{1,0:T(1,128)S(1)}, f32[1,1024]{1,0:T(1,128)S(1)}, u32[]{:S(2)}, u32[]{:S(2)}) %collective-permute-start) | collective-permute-done | bytes 4128 | tf_op jit(solution)/shard_map/ppermute | solution.py:406
  41.1 5.0 %all-to-all-done.1 = bf16[64,8,128]{2,1,0:T(8,128)(2,1)S(1)} async-done(((bf16[64,8,128]{2,1,0:T(8,128)(2,1)}), bf16[64,8,128]{2,1,0:T(8,128)(2,1)S(1)}, u32[]{:S(2)}, u32[]{:S(2)}) %all-to-all-start.1) | async-done | bytes 131104 | tf_op jit(solution)/shard_map/all_to_all | solution.py:402
  46.1 1.1 %adjoint.1 = bf16[8,2,48,128]{3,2,1,0:T(8,128)(2,1)S(1)} custom-call(s32[2]{0:T(128)S(1)} %pad_add_fusion.place_ref, bf16[2,256,128]{2,1,0:T(8,128)(2,1)S(1)} %bitcast.10, bf16[2,2,256,1024]{3,2,1,0:T(8,128)(2,1)S(1)} %get-tuple-element.12.tab_ref, f32[1,1024]{1,0:T(1,128)S(1)} %get-tuple-element.13.own_ref, f32[1,1024]{1,0:T(1,128)S(1)} %collective-permute-done.other_ref), custom_call_target="tpu_custom_call" | custom-call | tf_op jit(solution)/shard_map/adjoint/pallas_call | solution.py:349
  47.2 17.6 %all_to_all.15.sum_ref = bf16[8,2,48,128]{3,2,1,0:T(8,128)(2,1)S(1)} all-to-all(bf16[8,2,48,128]{3,2,1,0:T(8,128)(2,1)S(1)} %adjoint.1), channel_id=1, replica_groups=mesh['y'=8,'core'=2,'ma'=32] {'y'}, dimensions={0} | all-to-all | bytes 393216 | tf_op jit(solution)/shard_map/all_to_all | solution.py:408
  64.8 1.2 %final.1 = f32[2,48,128]{2,1,0:T(8,128)} custom-call(s32[2]{0:T(128)S(1)} %pad_add_fusion.place_ref, bf16[8,2,48,128]{3,2,1,0:T(8,128)(2,1)S(1)} %all_to_all.15.sum_ref, bf16[2,48,2048]{2,1,0:T(8,128)(2,1)S(1)} %bitcast.9, f32[6,128]{1,0:T(8,128)S(1)} %copy-done.5), custom_call_target="tpu_custom_call" | custom-call | tf_op jit(solution)/shard_map/final/pallas_call | solution.py:379
  (6 shorter events, 0.0 us)
Async XLA Ops:
  0.0 17.5 %copy-start.7 = (s32[64]{0:T(128)S(1)}, s32[64]{0:T(128)}, u32[]{:S(2)}) copy-start(s32[64]{0:T(128)} %m_ref.1) | copy-start | bytes 772
  0.0 26.3 %copy-start.1 = (f32[1,3,8,4096]{3,2,1,0:T(8,128)S(1)}, f32[1,3,8,4096]{3,2,1,0:T(8,128)}, u32[]{:S(2)}) copy-start(f32[1,3,8,4096]{3,2,1,0:T(8,128)} %mix_ref.1) | copy-start | bytes 1179652
  0.0 26.3 %copy-start.2 = (f32[1,2,8,4096]{3,2,1,0:T(8,128)S(1)}, f32[1,2,8,4096]{3,2,1,0:T(8,128)}, u32[]{:S(2)}) copy-start(f32[1,2,8,4096]{3,2,1,0:T(8,128)} %diag_ref.1) | copy-start | bytes 786436
  0.0 26.3 %copy-start.3 = (f32[1,8,4096]{2,1,0:T(8,128)S(1)}, f32[1,8,4096]{2,1,0:T(8,128)}, u32[]{:S(2)}) copy-start(f32[1,8,4096]{2,1,0:T(8,128)} %cross_ref.1) | copy-start | bytes 393220
  0.0 26.3 %copy-start.6 = (s32[8]{0:T(128)S(1)}, s32[8]{0:T(128)}, u32[]{:S(2)}) copy-start(s32[8]{0:T(128)} %ids_ref.1) | copy-start | bytes 100
  3.7 32.0 %copy-start.4 = (f32[1,2048]{1,0:T(1,128)S(1)}, f32[1,2048]{1,0:T(1,128)}, u32[]{:S(2)}) copy-start(f32[1,2048]{1,0:T(1,128)} %beam_ref.1) | copy-start | bytes 24580
  3.7 22.5 %all-to-all-start = ((bf16[32,8,128]{2,1,0:T(8,128)(2,1)}), bf16[32,8,128]{2,1,0:T(8,128)(2,1)S(1)}, u32[]{:S(2)}, u32[]{:S(2)}) async-start(bf16[32,8,128]{2,1,0:T(8,128)(2,1)} %bitcast.3), calls=%async_computation | async-start | bytes 131072 | tf_op jit(solution)/shard_map/all_to_all | solution.py:399
  29.3 16.8 %all-to-all-start.1 = ((bf16[64,8,128]{2,1,0:T(8,128)(2,1)}), bf16[64,8,128]{2,1,0:T(8,128)(2,1)S(1)}, u32[]{:S(2)}, u32[]{:S(2)}) async-start(bf16[64,8,128]{2,1,0:T(8,128)(2,1)} %bitcast.5), calls=%async_computation.1 | async-start | bytes 262144 | tf_op jit(solution)/shard_map/all_to_all | solution.py:402
  37.9 26.9 %copy-start = (bf16[2,2048,48]{1,2,0:T(8,128)(2,1)S(1)}, bf16[2,2048,48]{1,2,0:T(8,128)(2,1)}, u32[]{:S(2)}) copy-start(bf16[2,2048,48]{1,2,0:T(8,128)(2,1)} %param.9) | copy-start | bytes 1179652
  37.9 26.9 %copy-start.5 = (f32[6,128]{1,0:T(8,128)S(1)}, f32[6,128]{1,0:T(8,128)}, u32[]{:S(2)}) copy-start(f32[6,128]{1,0:T(8,128)} %prior_ref.1) | copy-start | bytes 9220
  37.9 3.2 %collective-permute-start = (f32[1,1024]{1,0:T(1,128)S(1)}, f32[1,1024]{1,0:T(1,128)S(1)}, u32[]{:S(2)}, u32[]{:S(2)}) collective-permute-start(f32[1,1024]{1,0:T(1,128)S(1)} %get-tuple-element.14), channel_id=1, source_target_pairs={{0,32},{32,0},{1,33},{33,1},{2,34},{34,2},{3,35},{35,3},{4,36},{36... | collective-permute-start | bytes 12296 | tf_op jit(solution)/shard_map/ppermute | solution.py:406

commit v4 on v3

--- a/solution.py
+++ b/solution.py
@@ -38,55 +38,46 @@
 SIGN = (-1.0, 1.0, 1.0, -1.0)
 
 
-CHUNKS = 4
-
-
-def synth_kernel(
-    coef_hbm, tab_hbm, beam_hbm, out_ref, coef_ref, tab_ref, beam_ref, rows_ref, nat_ref, cross_ref, sems
-):
+CHUNKS = 8
+
+
+def synth_kernel(coef_hbm, tab_hbm, beam_hbm, out_ref, coef_ref, tab_ref, beam_ref, rows_ref, nat_ref, cross_ref, sems):
     levels = coef_ref.shape[2]
     width = levels // CHUNKS
-    head = pltpu.make_async_copy(beam_hbm, beam_ref, sems.at[2, 0])
-    head.start()
+    heads = [
+        pltpu.make_async_copy(beam_hbm, beam_ref, sems.at[CHUNKS]),
+        pltpu.make_async_copy(coef_hbm, coef_ref, sems.at[CHUNKS + 1]),
+    ]
+    for head in heads:
+        head.start()
     copies = []
     for c in range(CHUNKS):
         at = pl.ds(c * width, width)
-        copies.append(
-            (
-                pltpu.make_async_copy(coef_hbm.at[:, :, at], coef_ref.at[:, :, at], sems.at[0, c]),
-                pltpu.make_async_copy(tab_hbm.at[:, :, :, at], tab_ref.at[c], sems.at[1, c]),
-            )
-        )
-        for copy in copies[c]:
-            copy.start()
-    rows_ref[:, :, COLS:, :] = jnp.zeros_like(rows_ref[:, :, COLS:, :])
-    head.wait()
-
-    def prepare(c):
-        copies[c][0].wait()
-        for s in range(2):
-            for j in range(c * width // 128, (c + 1) * width // 128):
-                at = slice(j * 128, (j + 1) * 128)
-                beamed = (coef_ref[s, :, at].astype(F32) * beam_ref[:, at]).astype(BF16)
-                rows_ref[s, 0, :COLS, at] = beamed
-                nat_ref[s, j] = beamed.astype(F32)
-                for k in range(4):
-                    value = nat_ref[s, j, pl.ds(3 - k, PAIRS, stride=4), :]
-                    cross_ref[s, j, pl.ds(k, PAIRS, stride=4), :] = SIGN[k] * value
-                rows_ref[s, 1, :COLS, at] = cross_ref[s, j].astype(BF16)
-
-    prepare(0)
+        copies.append(pltpu.make_async_copy(tab_hbm.at[:, :, :, at], tab_ref.at[c], sems.at[c]))
+        copies[-1].start()
+    rows_ref[...] = jnp.zeros_like(rows_ref)
+    for head in heads:
+        head.wait()
+    for s in range(2):
+        for j in range(levels // 128):
+            at = slice(j * 128, (j + 1) * 128)
+            beamed = (coef_ref[s, :, at].astype(F32) * beam_ref[:, at]).astype(BF16)
+            rows_ref[s, 0, 0:COLS, at] = beamed
+            nat_ref[s, j, :COLS, :] = beamed.astype(F32)
+            for k in range(4):
+                value = nat_ref[s, j, pl.ds(3 - k, PAIRS, stride=4), :]
+                cross_ref[s, j, pl.ds(k, PAIRS, stride=4), :] = SIGN[k] * value
+            rows_ref[s, 1, 0:COLS, at] = cross_ref[s, j].astype(BF16)
     total = [None, None]
     for c in range(CHUNKS):
-        copies[c][1].wait()
-        if c + 1 < CHUNKS:
-            prepare(c + 1)
+        copies[c].wait()
         for s in range(2):
             for which in range(2):
                 rows = rows_ref[s, which, :, c * width : (c + 1) * width]
                 part = dot(tab_ref[c, s, which], rows, NT)
                 total[s] = part if total[s] is None else total[s] + part
-    out_ref[...] = jnp.concatenate(total, 1).astype(BF16)
+    out = jnp.concatenate(total, 1)
+    out_ref[...] = out.astype(BF16)
 
 
 def synth(coeffs_t, tables, beam):
@@ -106,19 +97,28 @@
             pltpu.VMEM((2, 2, WIDE, levels), BF16),
             pltpu.VMEM((2, levels // 128, COLS, 128), F32),
             pltpu.VMEM((2, levels // 128, COLS, 128), F32),
-            pltpu.SemaphoreType.DMA((3, CHUNKS)),
+            pltpu.SemaphoreType.DMA((CHUNKS + 2,)),
         ],
         compiler_params=grant(12),
         name="synth",
     )(coeffs_t, tables, beam)
 
 
-def table_kernel(m_ref, out_ref, perm_ref):
+def odd_cycle(ids_ref, place):
+    odd = jnp.zeros(place.shape, F32)
+    for t in range(PER):
+        odd = jnp.where(place == t, (ids_ref[t] & 1).astype(F32), odd)
+    return odd
+
+
+def table_kernel(m_ref, ids_ref, out_ref, perm_ref, odd_row_ref, odd_lane_ref):
     row, col = iota(perm_ref.shape, 0), iota(perm_ref.shape, 1)
     field = row // PER
     upper = (field >= PAIRS).astype(jnp.int32)
     target = (row % PER) * (WIDE // 2) + 2 * (field - PAIRS * upper) + upper
     perm_ref[...] = jnp.where((col >> 1) == target, 1.0, 0.0).astype(BF16)
+    odd_row_ref[...] = odd_cycle(ids_ref, iota(odd_row_ref.shape, 0) % PER)
+    odd_lane_ref[...] = odd_cycle(ids_ref, iota(odd_lane_ref.shape, 1) % PER)
 
     quarter = PIX // 4
     row = iota((32, 128), 0)
@@ -164,32 +164,26 @@
     lax.fori_loop(0, quarter // 128, chunk, 0)
 
 
-def phase_table(m_values):
+def phase_table(m_values, cycle_ids):
+    rows = 2 * PAIRS * PER
     return pl.pallas_call(
         table_kernel,
         out_shape=(
             jax.ShapeDtypeStruct((256, PIX), BF16),
-            jax.ShapeDtypeStruct((2 * PAIRS * PER, WIDE * PER), BF16),
+            jax.ShapeDtypeStruct((rows, WIDE * PER), BF16),
+            jax.ShapeDtypeStruct((rows, 128), F32),
+            jax.ShapeDtypeStruct((8, rows), F32),
         ),
-        in_specs=[pl.BlockSpec(memory_space=pltpu.SMEM)],
-        out_specs=[pl.BlockSpec(memory_space=pltpu.VMEM)] * 2,
+        in_specs=[pl.BlockSpec(memory_space=pltpu.SMEM)] * 2,
+        out_specs=[pl.BlockSpec(memory_space=pltpu.VMEM)] * 4,
         cost_estimate=pl.CostEstimate(flops=8_000_000, bytes_accessed=2_097_152, transcendentals=0),
         compiler_params=grant(6),
         name="phase_table",
-    )(m_values)
-
-
-def by_cycle(values, place):
-    odd = jnp.zeros(place.shape, jnp.int32)
-    for t in range(PER):
-        odd = jnp.where(place == t, values[t], odd)
-    return odd == 1
-
-
-def pixel_kernel(
-    ids_ref, x_ref, tab_ref, perm_ref, mix_ref, diag_ref, cross_ref, out_ref, rows_ref, acc_ref
-):
-    parity = [ids_ref[t] & 1 for t in range(PER)]
+    )(m_values, cycle_ids)
+
+
+def pixel_kernel(x_ref, tab_ref, perm_ref, odd_row_ref, odd_lane_ref, *rest):
+    mix_ref, diag_ref, cross_ref, out_ref, rows_ref, acc_ref = rest
     lane = iota((32, 128), 1)
     left = lane < WIDE
     rows_ref[...] = x_ref[...].astype(F32)
@@ -206,13 +200,13 @@
     gathered = jnp.concatenate(tiles, 1).astype(BF16)
 
     lhs = dot(perm_ref[...], gathered, NT)
-    odd_row = by_cycle(parity, iota(lhs.shape, 0) % PER)
+    odd_row = odd_row_ref[...] > 0.5
     zero = jnp.zeros_like(lhs)
     lhs = jnp.concatenate(
         [jnp.where(odd_row, zero, lhs), jnp.where(odd_row, lhs, zero)], 1
     ).astype(BF16)
 
-    width = 2048
+    width = 4096
     for p in range(PIX // width):
         at = slice(p * width, (p + 1) * width)
         table = tab_ref[:, at]
@@ -244,7 +238,7 @@
         else:
             acc_ref[...] += part
 
-    odd_lane = by_cycle(parity, iota((128, acc_ref.shape[1]), 1) % PER)
+    odd_lane = jnp.concatenate([odd_lane_ref[...]] * 16, 0) > 0.5
     returned = jnp.where(odd_lane, acc_ref[128:, :], acc_ref[:128, :]).astype(BF16)
     spread = dot(returned, perm_ref[...], NN)
     for u in range(PER // 2):
@@ -261,24 +255,24 @@
     out_ref[1] = result
 
 
-def pixels(cycle_ids, arrived, table, perm, mixing, noise_diag, noise_cross):
+def pixels(arrived, helpers, mixing, noise_diag, noise_cross):
     vmem = pl.BlockSpec(memory_space=pltpu.VMEM)
     return pl.pallas_call(
         pixel_kernel,
         out_shape=jax.ShapeDtypeStruct((2, 256, 128), BF16),
-        in_specs=[pl.BlockSpec(memory_space=pltpu.SMEM)] + [vmem] * 6,
+        in_specs=[vmem] * 8,
         out_specs=vmem,
         scratch_shapes=[pltpu.VMEM((256, 128), F32), pltpu.VMEM((256, 2 * PAIRS * PER), F32)],
         compiler_params=grant(10),
         name="pixels",
-    )(cycle_ids, arrived, table, perm, mixing, noise_diag, noise_cross)
-
-
-def fetch_kernel(place_ref, tab_hbm, beam_ref, out_ref, own_ref, sent_ref, sems):
+    )(arrived, *helpers, mixing, noise_diag, noise_cross)
+
+
+def fetch_kernel(core_ref, band_ref, tab_hbm, beam_ref, out_ref, own_ref, sent_ref, sems):
     blocks = tab_hbm.shape[3] // 256
     copies = []
     for k in range(blocks):
-        source = pl.ds(pl.multiple_of(256 * k + 128 * place_ref[0], 128), 128)
+        source = pl.ds(pl.multiple_of(256 * k + 128 * core_ref[0], 128), 128)
         place = pl.ds(128 * k, 128)
         copies.append(
             pltpu.make_async_copy(
@@ -287,14 +281,14 @@
         )
         copies[-1].start()
         pair = [beam_ref[:, (2 * k + c) * 128 : (2 * k + c + 1) * 128] for c in range(2)]
-        second = place_ref[0] == 1
+        second = core_ref[0] == 1
         own_ref[:, 128 * k : 128 * (k + 1)] = jnp.where(second, pair[1], pair[0])
         sent_ref[:, 128 * k : 128 * (k + 1)] = jnp.where(second, pair[0], pair[1])
     for copy in copies:
         copy.wait()
 
 
-def fetch(place, tables, beam):
+def fetch(core, band, tables, beam):
     levels = tables.shape[3]
     hbm = pl.BlockSpec(memory_space=pltpu.HBM)
     vmem = pl.BlockSpec(memory_space=pltpu.VMEM)
@@ -305,19 +299,19 @@
             jax.ShapeDtypeStruct((1, levels // 2), F32),
             jax.ShapeDtypeStruct((1, levels // 2), F32),
         ),
-        in_specs=[pl.BlockSpec(memory_space=pltpu.SMEM), hbm, vmem],
+        in_specs=[pl.BlockSpec(memory_space=pltpu.SMEM)] * 2 + [hbm, vmem],
         out_specs=(vmem, vmem, vmem),
         scratch_shapes=[pltpu.SemaphoreType.DMA((levels // 256,))],
         compiler_params=grant(4),
         cost_estimate=pl.CostEstimate(flops=0, bytes_accessed=4_194_304, transcendentals=0),
         name="fetch",
-    )(place, tables, beam)
+    )(core, band, tables, beam)
 
 
 def adjoint_kernel(
-    place_ref, r_ref, tab_ref, own_ref, other_ref, out_ref, lhs_ref, plain_ref, cross_ref
+    core_ref, r_ref, tab_ref, own_ref, other_ref, out_ref, lhs_ref, plain_ref, cross_ref
 ):
-    for b, index in enumerate((place_ref[0], 1 - place_ref[0])):
+    for b, index in enumerate((core_ref[0], 1 - core_ref[0])):
         for h in range(2):
             half = slice(h * 128, (h + 1) * 128)
             plain_ref[b, h] = r_ref[index, half, :].astype(F32).T
@@ -342,7 +336,7 @@
                 out_ref[k * (width // 128) + h, s] = sums[:, h * 128 : (h + 1) * 128]
 
 
-def adjoint(place, returned, tables, own_beam, other_beam):
+def adjoint(core, returned, tables, own_beam, other_beam):
     cycles, levels = tables.shape[2:]
     blocks = levels // 128
     vmem = pl.BlockSpec(memory_space=pltpu.VMEM)
@@ -358,15 +352,15 @@
         ],
         compiler_params=grant(8),
         name="adjoint",
-    )(place, returned, tables, own_beam, other_beam)
-
-
-def final_kernel(place_ref, sum_ref, coef_ref, prior_ref, out_ref):
+    )(core, returned, tables, own_beam, other_beam)
+
+
+def final_kernel(band_ref, sum_ref, coef_ref, prior_ref, out_ref):
     kind = iota((COLS, 128), 0) % (4 * COMPS) // 2
     prior = jnp.zeros((COLS, 128), F32)
     for k in range(2 * COMPS):
         prior = jnp.where(kind == k, prior_ref[k : k + 1, :], prior)
-    at = pl.ds(pl.multiple_of(128 * place_ref[1], 128), 128)
+    at = pl.ds(pl.multiple_of(128 * band_ref[0], 128), 128)
     for s in range(2):
         total = prior * coef_ref[s, :, at].astype(F32)
         for y in range(sum_ref.shape[0]):
@@ -374,7 +368,7 @@
         out_ref[s] = total
 
 
-def final(place, gathered, coeffs_t, prior):
+def final(band, gathered, coeffs_t, prior):
     vmem = pl.BlockSpec(memory_space=pltpu.VMEM)
     return pl.pallas_call(
         final_kernel,
@@ -383,12 +377,13 @@
         out_specs=vmem,
         compiler_params=grant(4),
         name="final",
-    )(place, gathered, coeffs_t, prior)
+    )(band, gathered, coeffs_t, prior)
 
 
 def on_device(coeffs, tables, beam, mixing, noise_diag, noise_cross, prior, m_values, cycle_ids):
     core = lax.axis_index("core")
-    place = jnp.stack([core, 2 * lax.axis_index("y") + core]).astype(jnp.int32)
+    band = (2 * lax.axis_index("y") + core).astype(jnp.int32)[None]
+    core = core.astype(jnp.int32)[None]
     coeffs_t = coeffs.transpose(0, 2, 1)
     stored = pltpu.with_memory_space_constraint(tables, pltpu.HBM)
     spectra = synth(
@@ -397,16 +392,16 @@
         pltpu.with_memory_space_constraint(beam, pltpu.HBM),
     )
     arrived = lax.all_to_all(spectra.reshape(32, PER, 128), "ma", 0, 0, tiled=True)
-    table, perm = phase_table(m_values)
-    returned = pixels(cycle_ids, arrived.reshape(256, 128), table, perm, mixing, noise_diag, noise_cross)
+    helpers = phase_table(m_values, cycle_ids)
+    returned = pixels(arrived.reshape(256, 128), helpers, mixing, noise_diag, noise_cross)
     returned = lax.all_to_all(
         returned.reshape(64, PER, 128), ("core", "ma"), 0, 0, tiled=True
     ).reshape(2, 256, 128)
-    level_tables, own_beam, sent_beam = fetch(place, stored, beam)
+    level_tables, own_beam, sent_beam = fetch(core, band, stored, beam)
     other_beam = lax.ppermute(sent_beam, "core", [(0, 1), (1, 0)])
-    partial = adjoint(place, returned, level_tables, own_beam, other_beam)
+    partial = adjoint(core, returned, level_tables, own_beam, other_beam)
     gathered = lax.all_to_all(partial, "y", 0, 0, tiled=True)
-    return final(place, gathered, coeffs_t, prior).transpose(0, 2, 1)
+    return final(band, gathered, coeffs_t, prior).transpose(0, 2, 1)
 
 
 def solution(mesh):

time: 66.3 us -> 64.6 us (0.974)
  Pallas kernels: 13.7 us -> 11.5 us
where the time goes in v4:
time: 64.6 us; the launch traced here: 64.3 us
  starting transfers between devices  22.5 us (35%)
  blocking collectives  17.6 us (27%)
  waiting for transfers between devices  12.5 us (19%)
  Pallas kernels  11.5 us (18%)
    all_to_all x1, blocking collectives, on_device(): gathered = lax.all_to_all(partial, 'y', 0, 0, tiled=True)  17.6 us
    all_to_all x1, starting transfers between devices, on_device(): lax.all_to_all(spectra.reshape(32, PER, 128), 'ma', 0, 0, tiled=True)  13.7 us
    all_to_all x1, starting transfers between devices, on_device(): lax.all_to_all(returned.reshape(64, PER, 128), ('core', 'ma'), 0, 0, tile...  6.35 us
    all_to_all x1, waiting for transfers between devices, on_device(): lax.all_to_all(spectra.reshape(32, PER, 128), 'ma', 0, 0, tiled=True)  6.16 us
    all_to_all x1, waiting for transfers between devices, on_device(): lax.all_to_all(returned.reshape(64, PER, 128), ('core', 'ma'), 0, 0, tile...  5.58 us
    pallas_call x1, Pallas kernels, synth(): pl.pallas_call(synth_kernel, out_shape=jax.ShapeDtypeStruct((cycles, 128)...  3.64 us
    pallas_call x1, Pallas kernels, phase_table(): pl.pallas_call(table_kernel, out_shape=(jax.ShapeDtypeStruct((256, PIX),...  2.63 us
    ppermute x1, starting transfers between devices, on_device(): other_beam = lax.ppermute(sent_beam, 'core', [(0, 1), (1, 0)])  2.4 us
  transfers between devices with their start and end apart: 3, of which 3 were waited for; matrix products, arithmetic and copies ran while one was open for 0% of the time, Pallas kernels for 7%

profile of v4, /device:TPU:1, one launch (start us, length us, event | category | flops | bytes accessed | tf_op | source)
XLA Modules:
  0.0 64.3 jit_solution(11460009982016626012)
XLA Ops:
  0.0 0.0 copy-start.2
  0.0 0.0 copy-start.3
  0.0 3.6 %synth.1 = bf16[256,128]{1,0:T(8,128)(2,1)} custom-call(bf16[2,48,2048]{2,1,0:T(8,128)(2,1)} %bitcast.8, bf16[2,2,256,2048]{3,2,1,0:T(8,128)(2,1)} %tab_hbm.3, f32[1,2048]{1,0:T(1,128)} %beam_ref.1), custom_call_target="tpu_custom_call" | custom-call | tf_op jit(solution)/shard_map/synth/pallas_call | solution.py:88
  3.7 0.0 copy-start.4
  3.7 13.7 %all-to-all-start = ((bf16[32,8,128]{2,1,0:T(8,128)(2,1)}), bf16[32,8,128]{2,1,0:T(8,128)(2,1)S(1)}, u32[]{:S(2)}, u32[]{:S(2)}) async-start(bf16[32,8,128]{2,1,0:T(8,128)(2,1)} %bitcast.3), calls=%async_computation | async-start | bytes 131072 | tf_op jit(solution)/shard_map/all_to_all | solution.py:394
  17.4 0.0 copy-done.6
  17.4 0.0 copy-done.7
  17.4 2.6 %phase_table.1 = (bf16[256,4096]{1,0:T(8,128)(2,1)S(1)}, bf16[192,512]{1,0:T(8,128)(2,1)S(1)}, f32[192,128]{1,0:T(8,128)S(1)}, f32[8,192]{1,0:T(8,128)S(1)}) custom-call(s32[64]{0:T(128)S(1)} %copy-done.6, s32[8]{0:T(128)S(1)} %copy-done.7), custom_call_target="tpu_custom_call" | custom-call | flops 8000000 | bytes 2097152 | tf_op jit(solution)/shard_map/phase_table/pallas_call | solution.py:169
  20.1 6.2 %all-to-all-done = bf16[32,8,128]{2,1,0:T(8,128)(2,1)S(1)} async-done(((bf16[32,8,128]{2,1,0:T(8,128)(2,1)}), bf16[32,8,128]{2,1,0:T(8,128)(2,1)S(1)}, u32[]{:S(2)}, u32[]{:S(2)}) %all-to-all-start) | async-done | bytes 65568 | tf_op jit(solution)/shard_map/all_to_all | solution.py:394
  26.2 0.0 copy-done.1
  26.2 0.0 copy-done.2
  26.2 2.4 %pixels.1 = bf16[2,256,128]{2,1,0:T(8,128)(2,1)} custom-call(bf16[256,128]{1,0:T(8,128)(2,1)S(1)} %bitcast.11, bf16[256,4096]{1,0:T(8,128)(2,1)S(1)} %get-tuple-element.12.tab_ref, bf16[192,512]{1,0:T(8,128)(2,1)S(1)} %get-tuple-element.13.perm_ref, f32[192,128]{1,0:T(8,128)S(1)} %get-tuple-element.14.odd_row_ref, ...), custom_call_target="tpu_custom_call" | custom-call | tf_op jit(solution)/shard_map/pixels/pallas_call | solution.py:260
  28.6 6.3 %all-to-all-start.1 = ((bf16[64,8,128]{2,1,0:T(8,128)(2,1)}), bf16[64,8,128]{2,1,0:T(8,128)(2,1)S(1)}, u32[]{:S(2)}, u32[]{:S(2)}) async-start(bf16[64,8,128]{2,1,0:T(8,128)(2,1)} %bitcast.5), calls=%async_computation.1 | async-start | bytes 262144 | tf_op jit(solution)/shard_map/all_to_all | solution.py:397
  35.0 0.0 copy-done.4
  35.0 1.6 %fetch.1 = (bf16[2,2,256,1024]{3,2,1,0:T(8,128)(2,1)S(1)}, f32[1,1024]{1,0:T(1,128)S(1)}, f32[1,1024]{1,0:T(1,128)S(1)}) custom-call(s32[1]{0:T(128)} %bitcast.1.core_ref, s32[1]{0:T(128)} %bitcast.band_ref, bf16[2,2,256,2048]{3,2,1,0:T(8,128)(2,1)} %tab_hbm.3, f32[1,2048]{1,0:T(1,128)S(1)} %copy-done.4), custom_call_target="tpu_custom_call" | custom-call | bytes 4194304 | tf_op jit(solution)/shard_map/fetch/pallas_call | solution.py:295
  36.6 0.0 copy-start
  36.6 0.0 copy-start.5
  36.7 2.4 %collective-permute-start = (f32[1,1024]{1,0:T(1,128)S(1)}, f32[1,1024]{1,0:T(1,128)S(1)}, u32[]{:S(2)}, u32[]{:S(2)}) collective-permute-start(f32[1,1024]{1,0:T(1,128)S(1)} %get-tuple-element.18), channel_id=1, source_target_pairs={{0,32},{32,0},{1,33},{33,1},{2,34},{34,2},{3,35},{35,3},{4,36},{36... | collective-permute-start | bytes 12296 | tf_op jit(solution)/shard_map/ppermute | solution.py:401
  39.1 0.8 %collective-permute-done.other_ref = f32[1,1024]{1,0:T(1,128)S(1)} collective-permute-done((f32[1,1024]{1,0:T(1,128)S(1)}, f32[1,1024]{1,0:T(1,128)S(1)}, u32[]{:S(2)}, u32[]{:S(2)}) %collective-permute-start) | collective-permute-done | bytes 4128 | tf_op jit(solution)/shard_map/ppermute | solution.py:401
  39.9 5.6 %all-to-all-done.1 = bf16[64,8,128]{2,1,0:T(8,128)(2,1)S(1)} async-done(((bf16[64,8,128]{2,1,0:T(8,128)(2,1)}), bf16[64,8,128]{2,1,0:T(8,128)(2,1)S(1)}, u32[]{:S(2)}, u32[]{:S(2)}) %all-to-all-start.1) | async-done | bytes 131104 | tf_op jit(solution)/shard_map/all_to_all | solution.py:397
  45.4 0.6 adjoint.1
  46.0 17.6 %all_to_all.15.sum_ref = bf16[8,2,48,128]{3,2,1,0:T(8,128)(2,1)S(1)} all-to-all(bf16[8,2,48,128]{3,2,1,0:T(8,128)(2,1)S(1)} %adjoint.1), channel_id=1, replica_groups=mesh['y'=8,'core'=2,'ma'=32] {'y'}, dimensions={0} | all-to-all | bytes 393216 | tf_op jit(solution)/shard_map/all_to_all | solution.py:403
  63.6 0.0 copy-done.5
  63.6 0.7 %final.1 = f32[2,48,128]{2,1,0:T(8,128)} custom-call(s32[1]{0:T(128)} %bitcast.band_ref, bf16[8,2,48,128]{3,2,1,0:T(8,128)(2,1)S(1)} %all_to_all.15.sum_ref, bf16[2,48,2048]{2,1,0:T(8,128)(2,1)S(1)} %bitcast.9, f32[6,128]{1,0:T(8,128)S(1)} %copy-done.5), custom_call_target="tpu_custom_call" | custom-call | tf_op jit(solution)/shard_map/final/pallas_call | solution.py:373
  (5 shorter events, 0.0 us)
Async XLA Ops:
  0.0 17.4 %copy-start.6 = (s32[64]{0:T(128)S(1)}, s32[64]{0:T(128)}, u32[]{:S(2)}) copy-start(s32[64]{0:T(128)} %m_ref.1) | copy-start | bytes 772
  0.0 17.4 %copy-start.7 = (s32[8]{0:T(128)S(1)}, s32[8]{0:T(128)}, u32[]{:S(2)}) copy-start(s32[8]{0:T(128)} %ids_ref.1) | copy-start | bytes 100
  0.0 26.2 %copy-start.1 = (f32[1,3,8,4096]{3,2,1,0:T(8,128)S(1)}, f32[1,3,8,4096]{3,2,1,0:T(8,128)}, u32[]{:S(2)}) copy-start(f32[1,3,8,4096]{3,2,1,0:T(8,128)} %rest_0_.1) | copy-start | bytes 1179652
  0.0 26.2 %copy-start.2 = (f32[1,2,8,4096]{3,2,1,0:T(8,128)S(1)}, f32[1,2,8,4096]{3,2,1,0:T(8,128)}, u32[]{:S(2)}) copy-start(f32[1,2,8,4096]{3,2,1,0:T(8,128)} %rest_1_.1) | copy-start | bytes 786436
  0.0 26.2 %copy-start.3 = (f32[1,8,4096]{2,1,0:T(8,128)S(1)}, f32[1,8,4096]{2,1,0:T(8,128)}, u32[]{:S(2)}) copy-start(f32[1,8,4096]{2,1,0:T(8,128)} %rest_2_.1) | copy-start | bytes 393220
  3.7 31.3 %copy-start.4 = (f32[1,2048]{1,0:T(1,128)S(1)}, f32[1,2048]{1,0:T(1,128)}, u32[]{:S(2)}) copy-start(f32[1,2048]{1,0:T(1,128)} %beam_ref.1) | copy-start | bytes 24580
  3.7 22.5 %all-to-all-start = ((bf16[32,8,128]{2,1,0:T(8,128)(2,1)}), bf16[32,8,128]{2,1,0:T(8,128)(2,1)S(1)}, u32[]{:S(2)}, u32[]{:S(2)}) async-start(bf16[32,8,128]{2,1,0:T(8,128)(2,1)} %bitcast.3), calls=%async_computation | async-start | bytes 131072 | tf_op jit(solution)/shard_map/all_to_all | solution.py:394
  28.6 16.8 %all-to-all-start.1 = ((bf16[64,8,128]{2,1,0:T(8,128)(2,1)}), bf16[64,8,128]{2,1,0:T(8,128)(2,1)S(1)}, u32[]{:S(2)}, u32[]{:S(2)}) async-start(bf16[64,8,128]{2,1,0:T(8,128)(2,1)} %bitcast.5), calls=%async_computation.1 | async-start | bytes 262144 | tf_op jit(solution)/shard_map/all_to_all | solution.py:397
  36.6 27.0 %copy-start = (bf16[2,2048,48]{1,2,0:T(8,128)(2,1)S(1)}, bf16[2,2048,48]{1,2,0:T(8,128)(2,1)}, u32[]{:S(2)}) copy-start(bf16[2,2048,48]{1,2,0:T(8,128)(2,1)} %param.9) | copy-start | bytes 1179652
  36.6 26.9 %copy-start.5 = (f32[6,128]{1,0:T(8,128)S(1)}, f32[6,128]{1,0:T(8,128)}, u32[]{:S(2)}) copy-start(f32[6,128]{1,0:T(8,128)} %prior_ref.1) | copy-start | bytes 9220
  36.7 3.2 %collective-permute-start = (f32[1,1024]{1,0:T(1,128)S(1)}, f32[1,1024]{1,0:T(1,128)S(1)}, u32[]{:S(2)}, u32[]{:S(2)}) collective-permute-start(f32[1,1024]{1,0:T(1,128)S(1)} %get-tuple-element.18), channel_id=1, source_target_pairs={{0,32},{32,0},{1,33},{33,1},{2,34},{34,2},{3,35},{35,3},{4,36},{36... | collective-permute-start | bytes 12296 | tf_op jit(solution)/shard_map/ppermute | solution.py:401

commit v5 on v4

--- a/solution.py
+++ b/solution.py
@@ -17,6 +17,7 @@
 PAIRS = CHAINS * COMPS
 COLS = 4 * PAIRS
 WIDE = 64
+SPARE = WIDE - COLS
 PER = 8
 
 NT = (((1,), (1,)), ((), ()))
@@ -38,7 +39,7 @@
 SIGN = (-1.0, 1.0, 1.0, -1.0)
 
 
-CHUNKS = 8
+CHUNKS = 4
 
 
 def synth_kernel(coef_hbm, tab_hbm, beam_hbm, out_ref, coef_ref, tab_ref, beam_ref, rows_ref, nat_ref, cross_ref, sems):
@@ -111,7 +112,27 @@
     return odd
 
 
-def table_kernel(m_ref, ids_ref, out_ref, perm_ref, odd_row_ref, odd_lane_ref):
+def beam_rows(part, row):
+    lane, sub = iota((8, 128), 1), iota((8, 128), 0)
+    value = jnp.broadcast_to(row, (8, 128))
+    start = (part % 4) * 32
+    first = pltpu.roll(value, (128 + COLS - start) % 128, 1)
+    second = pltpu.roll(value, (128 + COLS + WIDE - SPARE - start) % 128, 1)
+    value = jnp.where(lane < WIDE, first, second)
+    value = jnp.where((lane & (WIDE - 1)) >= COLS, value, 0.0)
+    high = value.astype(BF16).astype(F32)
+    middle = (value - high).astype(BF16).astype(F32)
+    low = value - high - middle
+    return jnp.where(sub == 0, high, jnp.where(sub == 1, middle, jnp.where(sub == 2, low, 0.0)))
+
+
+def table_kernel(m_ref, ids_ref, band_ref, part_ref, beam_ref, *outs):
+    out_ref, perm_ref, odd_row_ref, odd_lane_ref, rows_ref = outs
+    part = part_ref[0]
+    for c in range(2):
+        at = pl.ds(pl.multiple_of(256 * (part // 4) + 128 * c, 128), 128)
+        rows_ref[c] = beam_rows(part, beam_ref[:, at])
+
     row, col = iota(perm_ref.shape, 0), iota(perm_ref.shape, 1)
     field = row // PER
     upper = (field >= PAIRS).astype(jnp.int32)
@@ -164,8 +185,10 @@
     lax.fori_loop(0, quarter // 128, chunk, 0)
 
 
-def phase_table(m_values, cycle_ids):
+def phase_table(m_values, cycle_ids, band, part, beam):
     rows = 2 * PAIRS * PER
+    smem = pl.BlockSpec(memory_space=pltpu.SMEM)
+    vmem = pl.BlockSpec(memory_space=pltpu.VMEM)
     return pl.pallas_call(
         table_kernel,
         out_shape=(
@@ -173,17 +196,26 @@
             jax.ShapeDtypeStruct((rows, WIDE * PER), BF16),
             jax.ShapeDtypeStruct((rows, 128), F32),
             jax.ShapeDtypeStruct((8, rows), F32),
+            jax.ShapeDtypeStruct((2, 8, 128), F32),
         ),
-        in_specs=[pl.BlockSpec(memory_space=pltpu.SMEM)] * 2,
-        out_specs=[pl.BlockSpec(memory_space=pltpu.VMEM)] * 4,
+        in_specs=[smem] * 4 + [vmem],
+        out_specs=[vmem] * 5,
         cost_estimate=pl.CostEstimate(flops=8_000_000, bytes_accessed=2_097_152, transcendentals=0),
         compiler_params=grant(6),
         name="phase_table",
-    )(m_values, cycle_ids)
-
-
-def pixel_kernel(x_ref, tab_ref, perm_ref, odd_row_ref, odd_lane_ref, *rest):
-    mix_ref, diag_ref, cross_ref, out_ref, rows_ref, acc_ref = rest
+    )(m_values, cycle_ids, band, part, beam)
+
+
+def pixel_kernel(core_ref, x_ref, tab_ref, perm_ref, odd_row_ref, odd_lane_ref, beam_ref, *rest):
+    mix_ref, diag_ref, cross_ref, levels_hbm, out_ref, levels_ref, rows_ref, acc_ref, sems = rest
+    copies = []
+    for k in range(levels_hbm.shape[3] // 256):
+        source = pl.ds(pl.multiple_of(256 * k + 128 * core_ref[0], 128), 128)
+        place = levels_ref.at[:, :, :, pl.ds(128 * k, 128)]
+        copies.append(
+            pltpu.make_async_copy(levels_hbm.at[:, :, :, source], place, sems.at[k])
+        )
+        copies[-1].start()
     lane = iota((32, 128), 1)
     left = lane < WIDE
     rows_ref[...] = x_ref[...].astype(F32)
@@ -250,71 +282,58 @@
         swapped = [pltpu.roll(v, WIDE, 1) for v in modes]
         rows_ref[pl.ds(2 * u, 32, stride=PER), :] = jnp.where(left, modes[0], swapped[1])
         rows_ref[pl.ds(2 * u + 1, 32, stride=PER), :] = jnp.where(left, swapped[0], modes[1])
-    result = rows_ref[...].astype(BF16)
-    out_ref[0] = result
-    out_ref[1] = result
-
-
-def pixels(arrived, helpers, mixing, noise_diag, noise_cross):
+    result = rows_ref[...].reshape(32, PER, 128)
+    for c in range(2):
+        out_ref[c] = (result + beam_ref[c][None]).reshape(256, 128).astype(BF16)
+    for copy in copies:
+        copy.wait()
+
+
+def pixels(core, arrived, helpers, mixing, noise_diag, noise_cross, tables):
+    levels = tables.shape[3] // 2
     vmem = pl.BlockSpec(memory_space=pltpu.VMEM)
+    smem = pl.BlockSpec(memory_space=pltpu.SMEM)
     return pl.pallas_call(
         pixel_kernel,
-        out_shape=jax.ShapeDtypeStruct((2, 256, 128), BF16),
-        in_specs=[vmem] * 8,
-        out_specs=vmem,
-        scratch_shapes=[pltpu.VMEM((256, 128), F32), pltpu.VMEM((256, 2 * PAIRS * PER), F32)],
+        out_shape=(
+            jax.ShapeDtypeStruct((2, 256, 128), BF16),
+            jax.ShapeDtypeStruct(tables.shape[:3] + (levels,), BF16),
+        ),
+        in_specs=[smem] + [vmem] * 9 + [pl.BlockSpec(memory_space=pltpu.HBM)],
+        out_specs=(vmem, vmem),
+        scratch_shapes=[
+            pltpu.VMEM((256, 128), F32),
+            pltpu.VMEM((256, 2 * PAIRS * PER), F32),
+            pltpu.SemaphoreType.DMA((levels // 128,)),
+        ],
         compiler_params=grant(10),
         name="pixels",
-    )(arrived, *helpers, mixing, noise_diag, noise_cross)
-
-
-def fetch_kernel(core_ref, band_ref, tab_hbm, beam_ref, out_ref, own_ref, sent_ref, sems):
-    blocks = tab_hbm.shape[3] // 256
-    copies = []
-    for k in range(blocks):
-        source = pl.ds(pl.multiple_of(256 * k + 128 * core_ref[0], 128), 128)
-        place = pl.ds(128 * k, 128)
-        copies.append(
-            pltpu.make_async_copy(
-                tab_hbm.at[:, :, :, source], out_ref.at[:, :, :, place], sems.at[k]
-            )
-        )
-        copies[-1].start()
-        pair = [beam_ref[:, (2 * k + c) * 128 : (2 * k + c + 1) * 128] for c in range(2)]
-        second = core_ref[0] == 1
-        own_ref[:, 128 * k : 128 * (k + 1)] = jnp.where(second, pair[1], pair[0])
-        sent_ref[:, 128 * k : 128 * (k + 1)] = jnp.where(second, pair[0], pair[1])
-    for copy in copies:
-        copy.wait()
-
-
-def fetch(core, band, tables, beam):
-    levels = tables.shape[3]
-    hbm = pl.BlockSpec(memory_space=pltpu.HBM)
-    vmem = pl.BlockSpec(memory_space=pltpu.VMEM)
-    return pl.pallas_call(
-        fetch_kernel,
-        out_shape=(
-            jax.ShapeDtypeStruct(tables.shape[:3] + (levels // 2,), BF16),
-            jax.ShapeDtypeStruct((1, levels // 2), F32),
-            jax.ShapeDtypeStruct((1, levels // 2), F32),
-        ),
-        in_specs=[pl.BlockSpec(memory_space=pltpu.SMEM)] * 2 + [hbm, vmem],
-        out_specs=(vmem, vmem, vmem),
-        scratch_shapes=[pltpu.SemaphoreType.DMA((levels // 256,))],
-        compiler_params=grant(4),
-        cost_estimate=pl.CostEstimate(flops=0, bytes_accessed=4_194_304, transcendentals=0),
-        name="fetch",
-    )(core, band, tables, beam)
+    )(core, arrived, *helpers, mixing, noise_diag, noise_cross, tables)
+
+
+def gather_beam(stage_ref, beam_ref):
+    parts = [stage_ref[pl.ds(i, 32, stride=PER), :] for i in range(3)]
+    stage_ref[:32, :] = parts[0] + parts[1] + parts[2]
+    lane = iota((8, 128), 1)
+    total = jnp.zeros((8, 128), F32)
+    for m in range(4):
+        value = stage_ref[pl.ds(m, 8, stride=4), :]
+        for i in range(2):
+            source, place = COLS + i * WIDE, m * 32 + i * SPARE
+            shift = (place - source) % 128
+            moved = pltpu.roll(value, shift, 1) if shift else value
+            total = jnp.where((lane >= place) & (lane < place + SPARE), moved, total)
+    beam_ref[...] = total
 
 
 def adjoint_kernel(
-    core_ref, r_ref, tab_ref, own_ref, other_ref, out_ref, lhs_ref, plain_ref, cross_ref
+    core_ref, r_ref, tab_ref, out_ref, lhs_ref, plain_ref, cross_ref, stage_ref, beam_ref
 ):
     for b, index in enumerate((core_ref[0], 1 - core_ref[0])):
+        stage_ref[b] = r_ref[index].astype(F32)
         for h in range(2):
             half = slice(h * 128, (h + 1) * 128)
-            plain_ref[b, h] = r_ref[index, half, :].astype(F32).T
+            plain_ref[b, h] = stage_ref[b, half, :].T
             for k in range(4):
                 value = plain_ref[b, h, pl.ds(3 - k, 32, stride=4), :]
                 cross_ref[b, h, pl.ds(k, 32, stride=4), :] = SIGN[k] * value
@@ -323,6 +342,7 @@
                 rows = slice(s * WIDE, s * WIDE + COLS)
                 lhs_ref[s, 0, at, half] = plain_ref[b, h, rows, :].astype(BF16)
                 lhs_ref[s, 1, at, half] = cross_ref[b, h, rows, :].astype(BF16)
+        gather_beam(stage_ref.at[b], beam_ref.at[b])
 
     width = 256
     for s in range(2):
@@ -331,28 +351,32 @@
             sums = dot(lhs_ref[s, 0], tab_ref[s, 0, :, at], NN) + dot(
                 lhs_ref[s, 1], tab_ref[s, 1, :, at], NN
             )
-            sums = (sums[:COLS] * own_ref[:, at] + sums[COLS:] * other_ref[:, at]).astype(BF16)
-            for h in range(width // 128):
-                out_ref[k * (width // 128) + h, s] = sums[:, h * 128 : (h + 1) * 128]
-
-
-def adjoint(core, returned, tables, own_beam, other_beam):
+            for h in range(2):
+                y = 2 * k + h
+                part = sums[:, h * 128 : (h + 1) * 128]
+                part = part[:COLS] * beam_ref[0, y : y + 1, :] + part[COLS:] * beam_ref[1, y : y + 1, :]
+                out_ref[y, s] = part.astype(BF16)
+
+
+def adjoint(core, returned, tables):
     cycles, levels = tables.shape[2:]
     blocks = levels // 128
     vmem = pl.BlockSpec(memory_space=pltpu.VMEM)
     return pl.pallas_call(
         adjoint_kernel,
         out_shape=jax.ShapeDtypeStruct((blocks, 2, COLS, 128), BF16),
-        in_specs=[pl.BlockSpec(memory_space=pltpu.SMEM)] + [vmem] * 4,
+        in_specs=[pl.BlockSpec(memory_space=pltpu.SMEM)] + [vmem] * 2,
         out_specs=vmem,
         scratch_shapes=[
             pltpu.VMEM((2, 2, 2 * COLS, cycles), BF16),
             pltpu.VMEM((2, 2, 128, 128), F32),
             pltpu.VMEM((2, 2, 128, 128), F32),
+            pltpu.VMEM((2, cycles, 128), F32),
+            pltpu.VMEM((2, blocks, 128), F32),
         ],
         compiler_params=grant(8),
         name="adjoint",
-    )(core, returned, tables, own_beam, other_beam)
+    )(core, returned, tables)
 
 
 def final_kernel(band_ref, sum_ref, coef_ref, prior_ref, out_ref):
@@ -392,14 +416,16 @@
         pltpu.with_memory_space_constraint(beam, pltpu.HBM),
     )
     arrived = lax.all_to_all(spectra.reshape(32, PER, 128), "ma", 0, 0, tiled=True)
-    helpers = phase_table(m_values, cycle_ids)
-    returned = pixels(arrived.reshape(256, 128), helpers, mixing, noise_diag, noise_cross)
+    part = lax.axis_index("ma").astype(jnp.int32)[None]
+    helpers = phase_table(m_values, cycle_ids, band, part, beam)
+    arrived = arrived.reshape(256, 128)
+    returned, level_tables = pixels(
+        core, arrived, helpers, mixing, noise_diag, noise_cross, stored
+    )
     returned = lax.all_to_all(
         returned.reshape(64, PER, 128), ("core", "ma"), 0, 0, tiled=True
     ).reshape(2, 256, 128)
-    level_tables, own_beam, sent_beam = fetch(core, band, stored, beam)
-    other_beam = lax.ppermute(sent_beam, "core", [(0, 1), (1, 0)])
-    partial = adjoint(core, returned, level_tables, own_beam, other_beam)
+    partial = adjoint(core, returned, level_tables)
     gathered = lax.all_to_all(partial, "y", 0, 0, tiled=True)
     return final(band, gathered, coeffs_t, prior).transpose(0, 2, 1)
 

time: 64.6 us -> 64.7 us (level)
  blocking collectives: 17.6 us -> 33.7 us
  starting transfers between devices: 22.5 us -> 13.7 us
  waiting for transfers between devices: 12.5 us -> 6.1 us
  Pallas kernels: 11.5 us -> 10.8 us
    all_to_all x0 -> x1, blocking collectives: none -> 16.1 us  [on_device(): lax.all_to_all(returned.reshape(64, PER, 128), ('core', 'ma'), 0, 0, tile...]
    all_to_all x1 -> x0, starting transfers between devices: 6.35 us -> none  [on_device(): lax.all_to_all(returned.reshape(64, PER, 128), ('core', 'ma'), 0, 0, tile...]
    all_to_all x1 -> x0, waiting for transfers between devices: 5.58 us -> none  [on_device(): lax.all_to_all(returned.reshape(64, PER, 128), ('core', 'ma'), 0, 0, tile...]
    ppermute x1 -> x0, starting transfers between devices: 2.4 us -> none  [on_device(): other_beam = lax.ppermute(sent_beam, 'core', [(0, 1), (1, 0)])]
    ppermute x1 -> x0, waiting for transfers between devices: 0.8 us -> none  [on_device(): other_beam = lax.ppermute(sent_beam, 'core', [(0, 1), (1, 0)])]
    pallas_call x2 -> x1, Pallas kernels: 4 us -> 3.27 us  [pixels(): pl.pallas_call(pixel_kernel, out_shape=(jax.ShapeDtypeStruct((2, 256, 128...]
  transfers between devices with their start and end apart: 3 -> 1, of which waited for: 3 -> 1; matrix products, arithmetic and copies ran while one was open for 0% -> 0% of each run, Pallas kernels for 7% -> 4%
where the time goes in v5:
time: 64.7 us; the launch traced here: 64.5 us
  blocking collectives  33.7 us (52%)
  starting transfers between devices  13.7 us (21%)
  Pallas kernels  10.8 us (17%)
  waiting for transfers between devices  6.1 us (9%)
    all_to_all x1, blocking collectives, on_device(): gathered = lax.all_to_all(partial, 'y', 0, 0, tiled=True)  17.6 us
    all_to_all x1, blocking collectives, on_device(): lax.all_to_all(returned.reshape(64, PER, 128), ('core', 'ma'), 0, 0, tile...  16.1 us
    all_to_all x1, starting transfers between devices, on_device(): lax.all_to_all(spectra.reshape(32, PER, 128), 'ma', 0, 0, tiled=True)  13.7 us
    all_to_all x1, waiting for transfers between devices, on_device(): lax.all_to_all(spectra.reshape(32, PER, 128), 'ma', 0, 0, tiled=True)  6.1 us
    pallas_call x1, Pallas kernels, synth(): pl.pallas_call(synth_kernel, out_shape=jax.ShapeDtypeStruct((cycles, 128)...  3.56 us
    pallas_call x1, Pallas kernels, pixels(): pl.pallas_call(pixel_kernel, out_shape=(jax.ShapeDtypeStruct((2, 256, 128...  3.27 us
    pallas_call x1, Pallas kernels, phase_table(): pl.pallas_call(table_kernel, out_shape=(jax.ShapeDtypeStruct((256, PIX),...  2.68 us
  transfers between devices with their start and end apart: 1, of which 1 were waited for; matrix products, arithmetic and copies ran while one was open for 0% of the time, Pallas kernels for 4%

profile of v5, /device:TPU:1, one launch (start us, length us, event | category | flops | bytes accessed | tf_op | source)
XLA Modules:
  0.0 64.5 jit_solution(8399687485589605464)
XLA Ops:
  0.0 0.0 copy-start.4
  0.0 0.0 copy-start.6
  0.0 0.0 copy-start.1
  0.0 0.0 copy-start.2
  0.0 0.0 copy-start.3
  0.0 3.6 %synth.1 = bf16[256,128]{1,0:T(8,128)(2,1)} custom-call(bf16[2,48,2048]{2,1,0:T(8,128)(2,1)} %bitcast.9, bf16[2,2,256,2048]{3,2,1,0:T(8,128)(2,1)} %rest_3_.1, f32[1,2048]{1,0:T(1,128)} %beam_ref.1), custom_call_target="tpu_custom_call" | custom-call | tf_op jit(solution)/shard_map/synth/pallas_call | solution.py:89
  3.6 13.7 %all-to-all-start = ((bf16[32,8,128]{2,1,0:T(8,128)(2,1)}), bf16[32,8,128]{2,1,0:T(8,128)(2,1)S(1)}, u32[]{:S(2)}, u32[]{:S(2)}) async-start(bf16[32,8,128]{2,1,0:T(8,128)(2,1)} %bitcast.3), calls=%async_computation | async-start | bytes 131072 | tf_op jit(solution)/shard_map/all_to_all | solution.py:418
  17.3 0.0 copy-done.4
  17.4 0.0 copy-done.6
  17.4 0.0 copy-done.7
  17.4 2.7 %phase_table.1 = (bf16[256,4096]{1,0:T(8,128)(2,1)S(1)}, bf16[192,512]{1,0:T(8,128)(2,1)S(1)}, f32[192,128]{1,0:T(8,128)S(1)}, f32[8,192]{1,0:T(8,128)S(1)}, f32[2,8,128]{2,1,0:T(8,128)S(1)}) custom-call(s32[64]{0:T(128)S(1)} %copy-done.6, s32[8]{0:T(128)S(1)} %copy-done.7, s32[1]{0:T(128)} %bitcast.band_ref, s32[1]{0:T(128)} %bitcast.5.part_ref, ...), custom_call_target="tpu_custom_call" | custom-call | flops 8000000 | bytes 2097152 | tf_op jit(solution)/shard_map/phase_table/pallas_call | solution.py:192
  20.1 6.1 %all-to-all-done = bf16[32,8,128]{2,1,0:T(8,128)(2,1)S(1)} async-done(((bf16[32,8,128]{2,1,0:T(8,128)(2,1)}), bf16[32,8,128]{2,1,0:T(8,128)(2,1)S(1)}, u32[]{:S(2)}, u32[]{:S(2)}) %all-to-all-start) | async-done | bytes 65568 | tf_op jit(solution)/shard_map/all_to_all | solution.py:418
  26.2 0.0 copy-done.1
  26.2 0.0 copy-done.2
  26.2 0.0 copy-done.3
  26.2 3.3 %pixels.1 = (bf16[2,256,128]{2,1,0:T(8,128)(2,1)S(1)}, bf16[2,2,256,1024]{3,2,1,0:T(8,128)(2,1)S(1)}) custom-call(s32[1]{0:T(128)} %bitcast.1.core_ref, bf16[256,128]{1,0:T(8,128)(2,1)S(1)} %bitcast.12, bf16[256,4096]{1,0:T(8,128)(2,1)S(1)} %get-tuple-element.12.tab_ref, bf16[192,512]{1,0:T(8,128)(2,1)S(1)} %get-tuple-element.13.perm_ref, ...), custom_call_target="tpu_custom_call" | custom-call | tf_op jit(solution)/shard_map/pixels/pallas_call | solution.py:296
  29.4 0.0 copy-start
  29.5 0.0 copy-start.5
  29.5 16.1 %all_to_all.15 = bf16[64,8,128]{2,1,0:T(8,128)(2,1)S(1)} all-to-all(bf16[64,8,128]{2,1,0:T(8,128)(2,1)S(1)} %bitcast.13), channel_id=1, replica_groups=mesh['y'=8,'core'=2,'ma'=32] {'core','ma'}, dimensions={0} | all-to-all | bytes 262144 | tf_op jit(solution)/shard_map/all_to_all | solution.py:425
  45.6 0.6 adjoint.1
  46.2 17.6 %all_to_all.16.sum_ref = bf16[8,2,48,128]{3,2,1,0:T(8,128)(2,1)S(1)} all-to-all(bf16[8,2,48,128]{3,2,1,0:T(8,128)(2,1)S(1)} %adjoint.1), channel_id=1, replica_groups=mesh['y'=8,'core'=2,'ma'=32] {'y'}, dimensions={0} | all-to-all | bytes 393216 | tf_op jit(solution)/shard_map/all_to_all | solution.py:429
  63.8 0.0 copy-done
  63.8 0.0 copy-done.5
  63.8 0.7 %final.1 = f32[2,48,128]{2,1,0:T(8,128)} custom-call(s32[1]{0:T(128)} %bitcast.band_ref, bf16[8,2,48,128]{3,2,1,0:T(8,128)(2,1)S(1)} %all_to_all.16.sum_ref, bf16[2,48,2048]{2,1,0:T(8,128)(2,1)S(1)} %bitcast.10, f32[6,128]{1,0:T(8,128)S(1)} %copy-done.5), custom_call_target="tpu_custom_call" | custom-call | tf_op jit(solution)/shard_map/final/pallas_call | solution.py:397
  (1 shorter events, 0.0 us)
Async XLA Ops:
  0.0 17.3 %copy-start.4 = (f32[1,2048]{1,0:T(1,128)S(1)}, f32[1,2048]{1,0:T(1,128)}, u32[]{:S(2)}) copy-start(f32[1,2048]{1,0:T(1,128)} %beam_ref.1) | copy-start | bytes 24580
  0.0 17.4 %copy-start.6 = (s32[64]{0:T(128)S(1)}, s32[64]{0:T(128)}, u32[]{:S(2)}) copy-start(s32[64]{0:T(128)} %m_ref.1) | copy-start | bytes 772
  0.0 17.4 %copy-start.7 = (s32[8]{0:T(128)S(1)}, s32[8]{0:T(128)}, u32[]{:S(2)}) copy-start(s32[8]{0:T(128)} %ids_ref.1) | copy-start | bytes 100
  0.0 26.1 %copy-start.1 = (f32[1,3,8,4096]{3,2,1,0:T(8,128)S(1)}, f32[1,3,8,4096]{3,2,1,0:T(8,128)}, u32[]{:S(2)}) copy-start(f32[1,3,8,4096]{3,2,1,0:T(8,128)} %rest_0_.1) | copy-start | bytes 1179652
  0.0 26.1 %copy-start.2 = (f32[1,2,8,4096]{3,2,1,0:T(8,128)S(1)}, f32[1,2,8,4096]{3,2,1,0:T(8,128)}, u32[]{:S(2)}) copy-start(f32[1,2,8,4096]{3,2,1,0:T(8,128)} %rest_1_.1) | copy-start | bytes 786436
  0.0 26.1 %copy-start.3 = (f32[1,8,4096]{2,1,0:T(8,128)S(1)}, f32[1,8,4096]{2,1,0:T(8,128)}, u32[]{:S(2)}) copy-start(f32[1,8,4096]{2,1,0:T(8,128)} %rest_2_.1) | copy-start | bytes 393220
  3.6 22.5 %all-to-all-start = ((bf16[32,8,128]{2,1,0:T(8,128)(2,1)}), bf16[32,8,128]{2,1,0:T(8,128)(2,1)S(1)}, u32[]{:S(2)}, u32[]{:S(2)}) async-start(bf16[32,8,128]{2,1,0:T(8,128)(2,1)} %bitcast.3), calls=%async_computation | async-start | bytes 131072 | tf_op jit(solution)/shard_map/all_to_all | solution.py:418
  29.4 34.4 %copy-start = (bf16[2,2048,48]{1,2,0:T(8,128)(2,1)S(1)}, bf16[2,2048,48]{1,2,0:T(8,128)(2,1)}, u32[]{:S(2)}) copy-start(bf16[2,2048,48]{1,2,0:T(8,128)(2,1)} %param.9) | copy-start | bytes 1179652
  29.5 34.3 %copy-start.5 = (f32[6,128]{1,0:T(8,128)S(1)}, f32[6,128]{1,0:T(8,128)}, u32[]{:S(2)}) copy-start(f32[6,128]{1,0:T(8,128)} %prior_ref.1) | copy-start | bytes 9220

commit v6 on v5

--- a/solution.py
+++ b/solution.py
@@ -126,8 +126,20 @@
     return jnp.where(sub == 0, high, jnp.where(sub == 1, middle, jnp.where(sub == 2, low, 0.0)))
 
 
-def table_kernel(m_ref, ids_ref, band_ref, part_ref, beam_ref, *outs):
-    out_ref, perm_ref, odd_row_ref, odd_lane_ref, rows_ref = outs
+def table_kernel(m_ref, ids_ref, core_ref, band_ref, part_ref, beam_ref, levels_hbm, *rest):
+    out_ref, perm_ref, odd_row_ref, odd_lane_ref, rows_ref, compact_hbm, held_ref, sems = rest
+    inward, outward = [], []
+    for k in range(levels_hbm.shape[3] // 256):
+        source = pl.ds(pl.multiple_of(256 * k + 128 * core_ref[0], 128), 128)
+        place = pl.ds(128 * k, 128)
+        held = held_ref.at[:, :, :, place]
+        inward.append(
+            pltpu.make_async_copy(levels_hbm.at[:, :, :, source], held, sems.at[0, k])
+        )
+        outward.append(
+            pltpu.make_async_copy(held, compact_hbm.at[:, :, :, place], sems.at[1, k])
+        )
+        inward[-1].start()
     part = part_ref[0]
     for c in range(2):
         at = pl.ds(pl.multiple_of(256 * (part // 4) + 128 * c, 128), 128)
@@ -182,11 +194,18 @@
                         out_ref[top : top + 32, at] = (value * scale).astype(BF16)
         return carry
 
-    lax.fori_loop(0, quarter // 128, chunk, 0)
-
-
-def phase_table(m_values, cycle_ids, band, part, beam):
+    lax.fori_loop(0, quarter // 256, chunk, 0)
+    for k in range(len(inward)):
+        inward[k].wait()
+        outward[k].start()
+    lax.fori_loop(quarter // 256, quarter // 128, chunk, 0)
+    for copy in outward:
+        copy.wait()
+
+
+def phase_table(m_values, cycle_ids, core, band, part, beam, tables):
     rows = 2 * PAIRS * PER
+    compact = tables.shape[:3] + (tables.shape[3] // 2,)
     smem = pl.BlockSpec(memory_space=pltpu.SMEM)
     vmem = pl.BlockSpec(memory_space=pltpu.VMEM)
     return pl.pallas_call(
@@ -197,24 +216,24 @@
             jax.ShapeDtypeStruct((rows, 128), F32),
             jax.ShapeDtypeStruct((8, rows), F32),
             jax.ShapeDtypeStruct((2, 8, 128), F32),
+            pltpu.HBM(compact, BF16),
         ),
-        in_specs=[smem] * 4 + [vmem],
-        out_specs=[vmem] * 5,
+        in_specs=[smem] * 5 + [vmem, pl.BlockSpec(memory_space=pltpu.HBM)],
+        out_specs=[vmem] * 5 + [pl.BlockSpec(memory_space=pltpu.HBM)],
+        scratch_shapes=[pltpu.VMEM(compact, BF16), pltpu.SemaphoreType.DMA((2, compact[3] // 128))],
         cost_estimate=pl.CostEstimate(flops=8_000_000, bytes_accessed=2_097_152, transcendentals=0),
-        compiler_params=grant(6),
+        compiler_params=grant(8),
         name="phase_table",
-    )(m_values, cycle_ids, band, part, beam)
-
-
-def pixel_kernel(core_ref, x_ref, tab_ref, perm_ref, odd_row_ref, odd_lane_ref, beam_ref, *rest):
-    mix_ref, diag_ref, cross_ref, levels_hbm, out_ref, levels_ref, rows_ref, acc_ref, sems = rest
+    )(m_values, cycle_ids, core, band, part, beam, tables)
+
+
+def pixel_kernel(x_ref, tab_ref, perm_ref, odd_row_ref, odd_lane_ref, beam_ref, *rest):
+    mix_ref, diag_ref, cross_ref, compact_hbm, out_ref, levels_ref, rows_ref, acc_ref, sems = rest
     copies = []
-    for k in range(levels_hbm.shape[3] // 256):
-        source = pl.ds(pl.multiple_of(256 * k + 128 * core_ref[0], 128), 128)
-        place = levels_ref.at[:, :, :, pl.ds(128 * k, 128)]
-        copies.append(
-            pltpu.make_async_copy(levels_hbm.at[:, :, :, source], place, sems.at[k])
-        )
+    for k in range(CHUNKS):
+        at = pl.ds(k * compact_hbm.shape[3] // CHUNKS, compact_hbm.shape[3] // CHUNKS)
+        source, place = compact_hbm.at[:, :, :, at], levels_ref.at[:, :, :, at]
+        copies.append(pltpu.make_async_copy(source, place, sems.at[k]))
         copies[-1].start()
     lane = iota((32, 128), 1)
     left = lane < WIDE
@@ -289,26 +308,25 @@
         copy.wait()
 
 
-def pixels(core, arrived, helpers, mixing, noise_diag, noise_cross, tables):
-    levels = tables.shape[3] // 2
+def pixels(arrived, helpers, mixing, noise_diag, noise_cross, compact):
     vmem = pl.BlockSpec(memory_space=pltpu.VMEM)
-    smem = pl.BlockSpec(memory_space=pltpu.SMEM)
+    hbm = pl.BlockSpec(memory_space=pltpu.HBM)
     return pl.pallas_call(
         pixel_kernel,
         out_shape=(
             jax.ShapeDtypeStruct((2, 256, 128), BF16),
-            jax.ShapeDtypeStruct(tables.shape[:3] + (levels,), BF16),
+            jax.ShapeDtypeStruct(compact.shape, compact.dtype),
         ),
-        in_specs=[smem] + [vmem] * 9 + [pl.BlockSpec(memory_space=pltpu.HBM)],
+        in_specs=[vmem] * 9 + [hbm],
         out_specs=(vmem, vmem),
         scratch_shapes=[
             pltpu.VMEM((256, 128), F32),
             pltpu.VMEM((256, 2 * PAIRS * PER), F32),
-            pltpu.SemaphoreType.DMA((levels // 128,)),
+            pltpu.SemaphoreType.DMA((CHUNKS,)),
         ],
         compiler_params=grant(10),
         name="pixels",
-    )(core, arrived, *helpers, mixing, noise_diag, noise_cross, tables)
+    )(arrived, *helpers, mixing, noise_diag, noise_cross, compact)
 
 
 def gather_beam(stage_ref, beam_ref):
@@ -417,10 +435,11 @@
     )
     arrived = lax.all_to_all(spectra.reshape(32, PER, 128), "ma", 0, 0, tiled=True)
     part = lax.axis_index("ma").astype(jnp.int32)[None]
-    helpers = phase_table(m_values, cycle_ids, band, part, beam)
+    *helpers, level_tables = phase_table(m_values, cycle_ids, core, band, part, beam, stored)
     arrived = arrived.reshape(256, 128)
+    level_tables = pltpu.with_memory_space_constraint(level_tables, pltpu.HBM)
     returned, level_tables = pixels(
-        core, arrived, helpers, mixing, noise_diag, noise_cross, stored
+        arrived, helpers, mixing, noise_diag, noise_cross, level_tables
     )
     returned = lax.all_to_all(
         returned.reshape(64, PER, 128), ("core", "ma"), 0, 0, tiled=True

time: 64.7 us -> 64.5 us (level)
  transfers between devices with their start and end apart: 1 -> 1, of which waited for: 1 -> 1; matrix products, arithmetic and copies ran while one was open for 0% -> 0% of each run, Pallas kernels for 4% -> 5%
where the time goes in v6:
time: 64.5 us; the launch traced here: 64.2 us
  blocking collectives  33.7 us (52%)
  starting transfers between devices  13.7 us (21%)
  Pallas kernels  11.1 us (17%)
  waiting for transfers between devices  5.51 us (9%)
    all_to_all x1, blocking collectives, on_device(): gathered = lax.all_to_all(partial, 'y', 0, 0, tiled=True)  17.6 us
    all_to_all x1, blocking collectives, on_device(): lax.all_to_all(returned.reshape(64, PER, 128), ('core', 'ma'), 0, 0, tile...  16.1 us
    all_to_all x1, starting transfers between devices, on_device(): lax.all_to_all(spectra.reshape(32, PER, 128), 'ma', 0, 0, tiled=True)  13.7 us
    all_to_all x1, waiting for transfers between devices, on_device(): lax.all_to_all(spectra.reshape(32, PER, 128), 'ma', 0, 0, tiled=True)  5.51 us
    pallas_call x1, Pallas kernels, synth(): pl.pallas_call(synth_kernel, out_shape=jax.ShapeDtypeStruct((cycles, 128)...  3.53 us
    pallas_call x1, Pallas kernels, phase_table(): pl.pallas_call(table_kernel, out_shape=(jax.ShapeDtypeStruct((256, PIX),...  3.23 us
    pallas_call x1, Pallas kernels, pixels(): pl.pallas_call(pixel_kernel, out_shape=(jax.ShapeDtypeStruct((2, 256, 128...  3.09 us
  transfers between devices with their start and end apart: 1, of which 1 were waited for; matrix products, arithmetic and copies ran while one was open for 0% of the time, Pallas kernels for 5%

profile of v6, /device:TPU:1, one launch (start us, length us, event | category | flops | bytes accessed | tf_op | source)
XLA Modules:
  0.0 64.2 jit_solution(1592030092347237932)
XLA Ops:
  0.0 0.0 copy-start.4
  0.0 0.0 copy-start.6
  0.0 3.5 %synth.1 = bf16[256,128]{1,0:T(8,128)(2,1)} custom-call(bf16[2,48,2048]{2,1,0:T(8,128)(2,1)} %bitcast.9, bf16[2,2,256,2048]{3,2,1,0:T(8,128)(2,1)} %levels_hbm.1, f32[1,2048]{1,0:T(1,128)} %beam_ref.1), custom_call_target="tpu_custom_call" | custom-call | tf_op jit(solution)/shard_map/synth/pallas_call | solution.py:89
  3.5 13.7 %all-to-all-start = ((bf16[32,8,128]{2,1,0:T(8,128)(2,1)}), bf16[32,8,128]{2,1,0:T(8,128)(2,1)S(1)}, u32[]{:S(2)}, u32[]{:S(2)}) async-start(bf16[32,8,128]{2,1,0:T(8,128)(2,1)} %bitcast.3), calls=%async_computation | async-start | bytes 131072 | tf_op jit(solution)/shard_map/all_to_all | solution.py:436
  17.3 0.0 copy-done.4
  17.3 0.0 copy-done.6
  17.3 0.0 copy-done.7
  17.3 0.0 copy-start.1
  17.3 0.0 copy-start.2
  17.3 0.0 copy-start.3
  17.3 3.2 %phase_table.1 = (bf16[256,4096]{1,0:T(8,128)(2,1)S(1)}, bf16[192,512]{1,0:T(8,128)(2,1)S(1)}, f32[192,128]{1,0:T(8,128)S(1)}, f32[8,192]{1,0:T(8,128)S(1)}, f32...) custom-call(s32[64]{0:T(128)S(1)} %copy-done.6, s32[8]{0:T(128)S(1)} %copy-done.7, s32[1]{0:T(128)} %bitcast.1.core_ref, ...), custom_call_target="tpu_custom_call" | custom-call | flops 8000000 | bytes 2097152 | tf_op jit(solution)/shard_map/phase_table/pallas_call | solution.py:211
  20.6 5.5 %all-to-all-done = bf16[32,8,128]{2,1,0:T(8,128)(2,1)S(1)} async-done(((bf16[32,8,128]{2,1,0:T(8,128)(2,1)}), bf16[32,8,128]{2,1,0:T(8,128)(2,1)S(1)}, u32[]{:S(2)}, u32[]{:S(2)}) %all-to-all-start) | async-done | bytes 65568 | tf_op jit(solution)/shard_map/all_to_all | solution.py:436
  26.1 0.0 copy-done.1
  26.1 0.0 copy-done.2
  26.1 0.0 copy-done.3
  26.1 3.1 %pixels.1 = (bf16[2,256,128]{2,1,0:T(8,128)(2,1)S(1)}, bf16[2,2,256,1024]{3,2,1,0:T(8,128)(2,1)S(1)}) custom-call(bf16[256,128]{1,0:T(8,128)(2,1)S(1)} %bitcast.12, bf16[256,4096]{1,0:T(8,128)(2,1)S(1)} %get-tuple-element.13.tab_ref, bf16[192,512]{1,0:T(8,128)(2,1)S(1)} %get-tuple-element.14.perm_ref, f32[192,128]{1,0:T(8,128)S(1)} %get-tuple-element.15.odd_row_ref, ...), custom_call_target="tpu_custom_call" | custom-call | tf_op jit(solution)/shard_map/pixels/pallas_call | solution.py:314
  29.2 0.0 copy-start
  29.2 0.0 copy-start.5
  29.2 16.1 %all_to_all.15 = bf16[64,8,128]{2,1,0:T(8,128)(2,1)S(1)} all-to-all(bf16[64,8,128]{2,1,0:T(8,128)(2,1)S(1)} %bitcast.13), channel_id=1, replica_groups=mesh['y'=8,'core'=2,'ma'=32] {'core','ma'}, dimensions={0} | all-to-all | bytes 262144 | tf_op jit(solution)/shard_map/all_to_all | solution.py:444
  45.4 0.6 adjoint.1
  46.0 17.6 %all_to_all.16.sum_ref = bf16[8,2,48,128]{3,2,1,0:T(8,128)(2,1)S(1)} all-to-all(bf16[8,2,48,128]{3,2,1,0:T(8,128)(2,1)S(1)} %adjoint.1), channel_id=1, replica_groups=mesh['y'=8,'core'=2,'ma'=32] {'y'}, dimensions={0} | all-to-all | bytes 393216 | tf_op jit(solution)/shard_map/all_to_all | solution.py:448
  63.5 0.0 copy-done
  63.5 0.0 copy-done.5
  63.5 0.7 %final.1 = f32[2,48,128]{2,1,0:T(8,128)} custom-call(s32[1]{0:T(128)} %bitcast.band_ref, bf16[8,2,48,128]{3,2,1,0:T(8,128)(2,1)S(1)} %all_to_all.16.sum_ref, bf16[2,48,2048]{2,1,0:T(8,128)(2,1)S(1)} %bitcast.10, f32[6,128]{1,0:T(8,128)S(1)} %copy-done.5), custom_call_target="tpu_custom_call" | custom-call | tf_op jit(solution)/shard_map/final/pallas_call | solution.py:415
  (1 shorter events, 0.0 us)
Async XLA Ops:
  0.0 17.3 %copy-start.4 = (f32[1,2048]{1,0:T(1,128)S(1)}, f32[1,2048]{1,0:T(1,128)}, u32[]{:S(2)}) copy-start(f32[1,2048]{1,0:T(1,128)} %beam_ref.1) | copy-start | bytes 24580
  0.0 17.3 %copy-start.6 = (s32[64]{0:T(128)S(1)}, s32[64]{0:T(128)}, u32[]{:S(2)}) copy-start(s32[64]{0:T(128)} %m_ref.1) | copy-start | bytes 772
  0.0 17.3 %copy-start.7 = (s32[8]{0:T(128)S(1)}, s32[8]{0:T(128)}, u32[]{:S(2)}) copy-start(s32[8]{0:T(128)} %ids_ref.1) | copy-start | bytes 100
  3.5 22.5 %all-to-all-start = ((bf16[32,8,128]{2,1,0:T(8,128)(2,1)}), bf16[32,8,128]{2,1,0:T(8,128)(2,1)S(1)}, u32[]{:S(2)}, u32[]{:S(2)}) async-start(bf16[32,8,128]{2,1,0:T(8,128)(2,1)} %bitcast.3), calls=%async_computation | async-start | bytes 131072 | tf_op jit(solution)/shard_map/all_to_all | solution.py:436
  17.3 8.8 %copy-start.1 = (f32[1,3,8,4096]{3,2,1,0:T(8,128)S(1)}, f32[1,3,8,4096]{3,2,1,0:T(8,128)}, u32[]{:S(2)}) copy-start(f32[1,3,8,4096]{3,2,1,0:T(8,128)} %rest_0_.1) | copy-start | bytes 1179652
  17.3 8.8 %copy-start.2 = (f32[1,2,8,4096]{3,2,1,0:T(8,128)S(1)}, f32[1,2,8,4096]{3,2,1,0:T(8,128)}, u32[]{:S(2)}) copy-start(f32[1,2,8,4096]{3,2,1,0:T(8,128)} %rest_1_.1) | copy-start | bytes 786436
  17.3 8.8 %copy-start.3 = (f32[1,8,4096]{2,1,0:T(8,128)S(1)}, f32[1,8,4096]{2,1,0:T(8,128)}, u32[]{:S(2)}) copy-start(f32[1,8,4096]{2,1,0:T(8,128)} %rest_2_.1) | copy-start | bytes 393220
  29.2 34.3 %copy-start = (bf16[2,2048,48]{1,2,0:T(8,128)(2,1)S(1)}, bf16[2,2048,48]{1,2,0:T(8,128)(2,1)}, u32[]{:S(2)}) copy-start(bf16[2,2048,48]{1,2,0:T(8,128)(2,1)} %param.9) | copy-start | bytes 1179652
  29.2 34.3 %copy-start.5 = (f32[6,128]{1,0:T(8,128)S(1)}, f32[6,128]{1,0:T(8,128)}, u32[]{:S(2)}) copy-start(f32[6,128]{1,0:T(8,128)} %prior_ref.1) | copy-start | bytes 9220

commit v7 on v6

--- a/solution.py
+++ b/solution.py
@@ -230,8 +230,8 @@
 def pixel_kernel(x_ref, tab_ref, perm_ref, odd_row_ref, odd_lane_ref, beam_ref, *rest):
     mix_ref, diag_ref, cross_ref, compact_hbm, out_ref, levels_ref, rows_ref, acc_ref, sems = rest
     copies = []
-    for k in range(CHUNKS):
-        at = pl.ds(k * compact_hbm.shape[3] // CHUNKS, compact_hbm.shape[3] // CHUNKS)
+    for k in range(2):
+        at = pl.ds(k * compact_hbm.shape[3] // 2, compact_hbm.shape[3] // 2)
         source, place = compact_hbm.at[:, :, :, at], levels_ref.at[:, :, :, at]
         copies.append(pltpu.make_async_copy(source, place, sems.at[k]))
         copies[-1].start()
@@ -322,7 +322,7 @@
         scratch_shapes=[
             pltpu.VMEM((256, 128), F32),
             pltpu.VMEM((256, 2 * PAIRS * PER), F32),
-            pltpu.SemaphoreType.DMA((CHUNKS,)),
+            pltpu.SemaphoreType.DMA((2,)),
         ],
         compiler_params=grant(10),
         name="pixels",

time: 64.5 us -> 64.4 us (level)
  no operation moved by 1% of the time
where the time goes in v7:
time: 64.4 us; the launch traced here: 64.1 us
  blocking collectives  33.7 us (52%)
  starting transfers between devices  13.7 us (21%)
  Pallas kernels  11 us (17%)
  waiting for transfers between devices  5.51 us (9%)
    all_to_all x1, blocking collectives, on_device(): gathered = lax.all_to_all(partial, 'y', 0, 0, tiled=True)  17.6 us
    all_to_all x1, blocking collectives, on_device(): lax.all_to_all(returned.reshape(64, PER, 128), ('core', 'ma'), 0, 0, tile...  16.1 us
    all_to_all x1, starting transfers between devices, on_device(): lax.all_to_all(spectra.reshape(32, PER, 128), 'ma', 0, 0, tiled=True)  13.7 us
    all_to_all x1, waiting for transfers between devices, on_device(): lax.all_to_all(spectra.reshape(32, PER, 128), 'ma', 0, 0, tiled=True)  5.51 us
    pallas_call x1, Pallas kernels, synth(): pl.pallas_call(synth_kernel, out_shape=jax.ShapeDtypeStruct((cycles, 128)...  3.53 us
    pallas_call x1, Pallas kernels, phase_table(): pl.pallas_call(table_kernel, out_shape=(jax.ShapeDtypeStruct((256, PIX),...  3.23 us
    pallas_call x1, Pallas kernels, pixels(): pl.pallas_call(pixel_kernel, out_shape=(jax.ShapeDtypeStruct((2, 256, 128...  2.96 us
  transfers between devices with their start and end apart: 1, of which 1 were waited for; matrix products, arithmetic and copies ran while one was open for 0% of the time, Pallas kernels for 5%

profile of v7, /device:TPU:1, one launch (start us, length us, event | category | flops | bytes accessed | tf_op | source)
XLA Modules:
  0.0 64.1 jit_solution(2758103209722454714)
XLA Ops:
  0.0 0.0 copy-start.4
  0.0 0.0 copy-start.6
  0.0 3.5 %synth.1 = bf16[256,128]{1,0:T(8,128)(2,1)} custom-call(bf16[2,48,2048]{2,1,0:T(8,128)(2,1)} %bitcast.9, bf16[2,2,256,2048]{3,2,1,0:T(8,128)(2,1)} %levels_hbm.1, f32[1,2048]{1,0:T(1,128)} %beam_ref.1), custom_call_target="tpu_custom_call" | custom-call | tf_op jit(solution)/shard_map/synth/pallas_call | solution.py:89
  3.5 13.7 %all-to-all-start = ((bf16[32,8,128]{2,1,0:T(8,128)(2,1)}), bf16[32,8,128]{2,1,0:T(8,128)(2,1)S(1)}, u32[]{:S(2)}, u32[]{:S(2)}) async-start(bf16[32,8,128]{2,1,0:T(8,128)(2,1)} %bitcast.3), calls=%async_computation | async-start | bytes 131072 | tf_op jit(solution)/shard_map/all_to_all | solution.py:436
  17.3 0.0 copy-done.4
  17.3 0.0 copy-done.6
  17.3 0.0 copy-done.7
  17.3 0.0 copy-start.1
  17.3 0.0 copy-start.2
  17.3 0.0 copy-start.3
  17.3 3.2 %phase_table.1 = (bf16[256,4096]{1,0:T(8,128)(2,1)S(1)}, bf16[192,512]{1,0:T(8,128)(2,1)S(1)}, f32[192,128]{1,0:T(8,128)S(1)}, f32[8,192]{1,0:T(8,128)S(1)}, f32...) custom-call(s32[64]{0:T(128)S(1)} %copy-done.6, s32[8]{0:T(128)S(1)} %copy-done.7, s32[1]{0:T(128)} %bitcast.1.core_ref, ...), custom_call_target="tpu_custom_call" | custom-call | flops 8000000 | bytes 2097152 | tf_op jit(solution)/shard_map/phase_table/pallas_call | solution.py:211
  20.6 5.5 %all-to-all-done = bf16[32,8,128]{2,1,0:T(8,128)(2,1)S(1)} async-done(((bf16[32,8,128]{2,1,0:T(8,128)(2,1)}), bf16[32,8,128]{2,1,0:T(8,128)(2,1)S(1)}, u32[]{:S(2)}, u32[]{:S(2)}) %all-to-all-start) | async-done | bytes 65568 | tf_op jit(solution)/shard_map/all_to_all | solution.py:436
  26.1 0.0 copy-done.1
  26.1 0.0 copy-done.2
  26.1 0.0 copy-done.3
  26.1 3.0 %pixels.1 = (bf16[2,256,128]{2,1,0:T(8,128)(2,1)S(1)}, bf16[2,2,256,1024]{3,2,1,0:T(8,128)(2,1)S(1)}) custom-call(bf16[256,128]{1,0:T(8,128)(2,1)S(1)} %bitcast.12, bf16[256,4096]{1,0:T(8,128)(2,1)S(1)} %get-tuple-element.13.tab_ref, bf16[192,512]{1,0:T(8,128)(2,1)S(1)} %get-tuple-element.14.perm_ref, f32[192,128]{1,0:T(8,128)S(1)} %get-tuple-element.15.odd_row_ref, ...), custom_call_target="tpu_custom_call" | custom-call | tf_op jit(solution)/shard_map/pixels/pallas_call | solution.py:314
  29.1 0.0 copy-start
  29.1 0.0 copy-start.5
  29.1 16.1 %all_to_all.15 = bf16[64,8,128]{2,1,0:T(8,128)(2,1)S(1)} all-to-all(bf16[64,8,128]{2,1,0:T(8,128)(2,1)S(1)} %bitcast.13), channel_id=1, replica_groups=mesh['y'=8,'core'=2,'ma'=32] {'core','ma'}, dimensions={0} | all-to-all | bytes 262144 | tf_op jit(solution)/shard_map/all_to_all | solution.py:444
  45.2 0.6 adjoint.1
  45.8 17.6 %all_to_all.16.sum_ref = bf16[8,2,48,128]{3,2,1,0:T(8,128)(2,1)S(1)} all-to-all(bf16[8,2,48,128]{3,2,1,0:T(8,128)(2,1)S(1)} %adjoint.1), channel_id=1, replica_groups=mesh['y'=8,'core'=2,'ma'=32] {'y'}, dimensions={0} | all-to-all | bytes 393216 | tf_op jit(solution)/shard_map/all_to_all | solution.py:448
  63.4 0.0 copy-done
  63.4 0.0 copy-done.5
  63.4 0.7 %final.1 = f32[2,48,128]{2,1,0:T(8,128)} custom-call(s32[1]{0:T(128)} %bitcast.band_ref, bf16[8,2,48,128]{3,2,1,0:T(8,128)(2,1)S(1)} %all_to_all.16.sum_ref, bf16[2,48,2048]{2,1,0:T(8,128)(2,1)S(1)} %bitcast.10, f32[6,128]{1,0:T(8,128)S(1)} %copy-done.5), custom_call_target="tpu_custom_call" | custom-call | tf_op jit(solution)/shard_map/final/pallas_call | solution.py:415
  (1 shorter events, 0.0 us)
Async XLA Ops:
  0.0 17.3 %copy-start.4 = (f32[1,2048]{1,0:T(1,128)S(1)}, f32[1,2048]{1,0:T(1,128)}, u32[]{:S(2)}) copy-start(f32[1,2048]{1,0:T(1,128)} %beam_ref.1) | copy-start | bytes 24580
  0.0 17.3 %copy-start.6 = (s32[64]{0:T(128)S(1)}, s32[64]{0:T(128)}, u32[]{:S(2)}) copy-start(s32[64]{0:T(128)} %m_ref.1) | copy-start | bytes 772
  0.0 17.3 %copy-start.7 = (s32[8]{0:T(128)S(1)}, s32[8]{0:T(128)}, u32[]{:S(2)}) copy-start(s32[8]{0:T(128)} %ids_ref.1) | copy-start | bytes 100
  3.5 22.5 %all-to-all-start = ((bf16[32,8,128]{2,1,0:T(8,128)(2,1)}), bf16[32,8,128]{2,1,0:T(8,128)(2,1)S(1)}, u32[]{:S(2)}, u32[]{:S(2)}) async-start(bf16[32,8,128]{2,1,0:T(8,128)(2,1)} %bitcast.3), calls=%async_computation | async-start | bytes 131072 | tf_op jit(solution)/shard_map/all_to_all | solution.py:436
  17.3 8.8 %copy-start.1 = (f32[1,3,8,4096]{3,2,1,0:T(8,128)S(1)}, f32[1,3,8,4096]{3,2,1,0:T(8,128)}, u32[]{:S(2)}) copy-start(f32[1,3,8,4096]{3,2,1,0:T(8,128)} %rest_0_.1) | copy-start | bytes 1179652
  17.3 8.8 %copy-start.2 = (f32[1,2,8,4096]{3,2,1,0:T(8,128)S(1)}, f32[1,2,8,4096]{3,2,1,0:T(8,128)}, u32[]{:S(2)}) copy-start(f32[1,2,8,4096]{3,2,1,0:T(8,128)} %rest_1_.1) | copy-start | bytes 786436
  17.3 8.8 %copy-start.3 = (f32[1,8,4096]{2,1,0:T(8,128)S(1)}, f32[1,8,4096]{2,1,0:T(8,128)}, u32[]{:S(2)}) copy-start(f32[1,8,4096]{2,1,0:T(8,128)} %rest_2_.1) | copy-start | bytes 393220
  29.1 34.3 %copy-start = (bf16[2,2048,48]{1,2,0:T(8,128)(2,1)S(1)}, bf16[2,2048,48]{1,2,0:T(8,128)(2,1)}, u32[]{:S(2)}) copy-start(bf16[2,2048,48]{1,2,0:T(8,128)(2,1)} %param.9) | copy-start | bytes 1179652
  29.1 34.3 %copy-start.5 = (f32[6,128]{1,0:T(8,128)S(1)}, f32[6,128]{1,0:T(8,128)}, u32[]{:S(2)}) copy-start(f32[6,128]{1,0:T(8,128)} %prior_ref.1) | copy-start | bytes 9220
